TPU v7x, 32 devices: a whole 2x2x4 slice. The times are simulated.
32 devices in a mesh: expert: 8 (over z, y), tensor: 4 (over x, core).
Axes of the slice: x: 2, y: 2, z: 4, core: 2. Of those that a mesh axis runs over, the one named last changes fastest.
Arguments:
- block_input: bfloat16 [1576, 768], P('expert'), may hold values from -6.5 to 6.5
- attn_gain: float32 [768], replicated, may hold values from 0.1 to 1.9
- attn_proj: bfloat16 [768, 3, 768], P(None, None, 'tensor'), may hold values from -9.021098 to 9.021098
- attn_merge: bfloat16 [768, 768], P('tensor'), may hold values from -1.75 to 1.75
- mixer_gain: float32 [768], replicated, may hold values from 0.1 to 1.9
- router_weight: bfloat16 [768, 4], replicated, may hold values from -0.21875 to 0.21875
- expert_up: bfloat16 [8, 768, 1536], P('expert', None, 'tensor'), may hold values from -0.21875 to 0.21875
- expert_down: bfloat16 [8, 1536, 768], P('expert', 'tensor'), may hold values from -0.109375 to 0.109375
- routes: int32 [1576, 2], P('expert'), may hold values from 0 to 3, all different within a row; in each aligned block of 197 rows (0 to 196, 197 to 393, ...) at most 192 rows name the same one
- keep_mask: int32 [1576, 2], P('expert'), may hold values 0 or 1
- out_grad: bfloat16 [1576, 768], P('expert'), may hold values from -18.5 to 18.5
Outputs:
- block_output: bfloat16 [1576, 768], P('expert')
- input_grad: float32 [1576, 768], P('expert')
- attn_gain_grad: float32 [768], replicated
- attn_proj_grad: float32 [768, 3, 768], P(None, None, 'tensor')
- attn_merge_grad: float32 [768, 768], P('tensor')
- mixer_gain_grad: float32 [768], replicated
- router_grad: float32 [768, 4], replicated
- expert_up_grad: float32 [8, 768, 1536], P('expert', None, 'tensor')
- expert_down_grad: float32 [8, 1536, 768], P('expert', 'tensor')
Inputs may be any that keep to these rules, and one draw needn't show every extreme that they name: `routes`: in each aligned block of 197 rows no expert is named by more than 192 rows, a bound that some block reaches; a row names two different experts.
All inputs are finite; a program needn't handle non-finite values. No bound on the sum of `keep_mask` on one device may be relied on, other than what follows from the above.
Results may differ from a plain program's by a relative error of at most 0.028.
The roundings to bfloat16 on the way count: a program that leaves them out, or rounds other values in their place, can miss the bound.
Values may be sent and summed in bfloat16 or wider, within the bound.
A program may use at most 128 MiB of HBM per device.

v0:
```python
import jax
import jax.numpy as jnp
from jax import lax
from jax.sharding import PartitionSpec as P

D = 768
SEQ = 197
PAIR = 2
IMG_DEV = 1
HEAD = 64
TOK_DEV = 197


EPS = 1e-06
ROOT_HALF = 0.7071067811865476
INV_ROOT_TAU = 0.3989422804014327


def norm_parts(values):
    center = values - jnp.mean(values, axis=-1, keepdims=True)
    inverse = lax.rsqrt(jnp.mean(center * center, axis=-1, keepdims=True) + EPS)
    return (center * inverse, inverse)


def norm_back(upstream, normed, inverse, gain):
    scaled = upstream * gain
    return inverse * (
        scaled
        - jnp.mean(scaled, axis=-1, keepdims=True)
        - normed * jnp.mean(scaled * normed, axis=-1, keepdims=True)
    )


def gelu_value(pre_act):
    return 0.5 * pre_act * (1.0 + lax.erf(pre_act * ROOT_HALF))


def gelu_slope(pre_act):
    return (
        0.5 * (1.0 + lax.erf(pre_act * ROOT_HALF))
        + pre_act * jnp.exp(-0.5 * pre_act * pre_act) * INV_ROOT_TAU
    )


def slot_table(routes, keep_mask, experts):
    labels = jnp.arange(experts, dtype=jnp.int32)
    chosen = routes[:, :, None] == labels[None, None, :]
    hits = jnp.where(chosen & (keep_mask[:, :, None] > 0), 1, 0).astype(jnp.int32)
    per_token = jnp.sum(hits, axis=1)
    before = jnp.cumsum(per_token, axis=0) - per_token
    return jnp.sum(jnp.where(chosen, before[:, None, :], 0), axis=2)


def spread_rows(slot_rows, experts, capacity):
    width = slot_rows.shape[-1]
    paired = jnp.broadcast_to(
        slot_rows.reshape(experts, 1, capacity, width), (experts, PAIR, capacity, width)
    )
    paired = paired.reshape(experts * PAIR, capacity, width)
    arrived = lax.all_to_all(paired, "expert", split_axis=0, concat_axis=0, tiled=True)
    return arrived.reshape(-1, width)


def return_rows(partial_terms, experts, capacity):
    width = partial_terms.shape[-1]
    sent_rows = partial_terms.astype(jnp.bfloat16).reshape(experts * PAIR, capacity, width)
    landed = lax.all_to_all(sent_rows, "expert", split_axis=0, concat_axis=0, tiled=True).astype(
        jnp.float32
    )
    return jnp.sum(landed.reshape(experts, PAIR, capacity, width), axis=1).reshape(
        experts * capacity, width
    )


def on_device(
    block_input,
    attn_gain,
    attn_proj,
    attn_merge,
    mixer_gain,
    router_weight,
    expert_up,
    expert_down,
    routes,
    keep_mask,
    out_grad,
):
    experts = lax.axis_size("expert") // PAIR
    capacity = max(8, 4 * TOK_DEV // experts // 8 * 8)
    local_width = attn_proj.shape[2]
    heads_here = local_width // HEAD
    score_scale = HEAD ** (-0.5)
    tokens = block_input.shape[0]
    wide_input = block_input.astype(jnp.float32)
    normed_one, inverse_one = norm_parts(wide_input)
    first_in = (normed_one * attn_gain).astype(jnp.bfloat16)
    proj = jnp.einsum(
        "td,dce->tce", first_in, attn_proj, preferred_element_type=jnp.float32
    ).astype(jnp.bfloat16)
    head_grid = proj.reshape(IMG_DEV, SEQ, 3, heads_here, HEAD)
    queries = head_grid[:, :, 0]
    key_heads = head_grid[:, :, 1]
    value_heads = head_grid[:, :, 2]
    raw = (
        jnp.einsum("bqhe,bkhe->bhqk", queries, key_heads, preferred_element_type=jnp.float32)
        * score_scale
    )
    row_top = jnp.max(raw, axis=-1)
    log_total = row_top + jnp.log(jnp.sum(jnp.exp(raw - row_top[..., None]), axis=-1))
    attn_probs = jnp.exp(raw - log_total[..., None]).astype(jnp.bfloat16)
    heads_out = jnp.einsum(
        "bhqk,bkhe->bqhe", attn_probs, value_heads, preferred_element_type=jnp.float32
    )
    heads_out = heads_out.astype(jnp.bfloat16).reshape(tokens, local_width)
    merge_terms = jnp.dot(heads_out, attn_merge, preferred_element_type=jnp.float32)
    middle = wide_input + lax.psum(merge_terms.astype(jnp.bfloat16), "tensor").astype(jnp.float32)
    normed_two, inverse_two = norm_parts(middle)
    second_in = (normed_two * mixer_gain).astype(jnp.bfloat16)
    logits = jnp.dot(second_in, router_weight, preferred_element_type=jnp.float32)
    labels = jnp.arange(experts, dtype=jnp.int32)
    first_hot = (routes[:, 0:1] == labels[None, :]).astype(jnp.float32)
    second_hot = (routes[:, 1:2] == labels[None, :]).astype(jnp.float32)
    gate_first = jax.nn.sigmoid(jnp.sum(logits * (first_hot - second_hot), axis=1))
    kept = keep_mask.astype(jnp.float32)
    gate_weights = jnp.stack([gate_first, 1.0 - gate_first], axis=1) * kept
    slots = slot_table(routes, keep_mask, experts)
    live_mask = keep_mask > 0
    target = jnp.where(live_mask, routes * capacity + slots, experts * capacity).reshape(-1)
    source = jnp.where(live_mask, routes * capacity + slots, 0)
    send_rows = (
        jnp.zeros((experts * capacity, D), jnp.bfloat16)
        .at[target]
        .set(jnp.repeat(second_in, 2, axis=0), mode="drop")
    )
    arrived = spread_rows(send_rows, experts, capacity)
    pre_act = jnp.dot(arrived, expert_up[0], preferred_element_type=jnp.float32)
    hidden = gelu_value(pre_act).astype(jnp.bfloat16)
    partial_terms = jnp.dot(hidden, expert_down[0], preferred_element_type=jnp.float32)
    expert_rows = return_rows(partial_terms, experts, capacity)
    picked = expert_rows[source] * kept[:, :, None]
    mixed_rows = jnp.sum(gate_weights[:, :, None] * picked, axis=1)
    moe = lax.psum(mixed_rows.astype(jnp.bfloat16), "tensor").astype(jnp.float32)
    block_output = (middle + moe).astype(jnp.bfloat16)
    grad_wide = out_grad.astype(jnp.float32)
    d_rows = (
        (gate_weights[:, :, None] * grad_wide[:, None, :])
        .astype(jnp.bfloat16)
        .reshape(tokens * 2, D)
    )
    d_send = jnp.zeros((experts * capacity, D), jnp.bfloat16).at[target].set(d_rows, mode="drop")
    d_arrived = spread_rows(d_send, experts, capacity)
    d_hidden = lax.dot_general(
        d_arrived, expert_down[0], (((1,), (1,)), ((), ())), preferred_element_type=jnp.float32
    )
    down_local = lax.dot_general(
        hidden, d_arrived, (((0,), (0,)), ((), ())), preferred_element_type=jnp.float32
    )
    d_pre = (d_hidden * gelu_slope(pre_act)).astype(jnp.bfloat16)
    up_local = lax.dot_general(
        arrived, d_pre, (((0,), (0,)), ((), ())), preferred_element_type=jnp.float32
    )
    d_terms = lax.dot_general(
        d_pre, expert_up[0], (((1,), (1,)), ((), ())), preferred_element_type=jnp.float32
    )
    d_back = return_rows(d_terms, experts, capacity)
    d_picked = jnp.sum(d_back[source] * kept[:, :, None], axis=1)
    dots_part = jnp.sum(picked * grad_wide[:, None, :], axis=2)
    d_moe, gate_dots = (
        lax.psum(d_picked.astype(jnp.bfloat16), "tensor").astype(jnp.float32),
        lax.psum(dots_part.astype(jnp.bfloat16), "tensor").astype(jnp.float32),
    )
    d_gates = gate_dots * kept
    d_diff = (d_gates[:, 0] - d_gates[:, 1]) * gate_first * (1.0 - gate_first)
    d_logits = (d_diff[:, None] * (first_hot - second_hot)).astype(jnp.bfloat16)
    router_part = lax.dot_general(
        second_in, d_logits, (((0,), (0,)), ((), ())), preferred_element_type=jnp.float32
    )
    d_second = d_moe + lax.dot_general(
        d_logits, router_weight, (((1,), (1,)), ((), ())), preferred_element_type=jnp.float32
    )
    mixer_part = jnp.sum(d_second * normed_two, axis=0)
    d_middle = grad_wide + norm_back(d_second, normed_two, inverse_two, mixer_gain)
    d_low = d_middle.astype(jnp.bfloat16)
    merge_local = lax.dot_general(
        heads_out, d_low, (((0,), (0,)), ((), ())), preferred_element_type=jnp.float32
    )
    d_heads = lax.dot_general(
        d_low, attn_merge, (((1,), (1,)), ((), ())), preferred_element_type=jnp.float32
    ).astype(jnp.bfloat16)
    d_grid = d_heads.reshape(IMG_DEV, SEQ, heads_here, HEAD)
    out_grid = heads_out.reshape(IMG_DEV, SEQ, heads_here, HEAD)
    delta = jnp.einsum("bqhe,bqhe->bhq", d_grid, out_grid, preferred_element_type=jnp.float32)
    raw_again = (
        jnp.einsum("bqhe,bkhe->bhqk", queries, key_heads, preferred_element_type=jnp.float32)
        * score_scale
    )
    probs_wide = jnp.exp(raw_again - log_total[..., None])
    probs_low = probs_wide.astype(jnp.bfloat16)
    d_probs = jnp.einsum("bqhe,bkhe->bhqk", d_grid, value_heads, preferred_element_type=jnp.float32)
    d_raw = (probs_wide * (d_probs - delta[..., None]) * score_scale).astype(jnp.bfloat16)
    d_queries = jnp.einsum("bhqk,bkhe->bqhe", d_raw, key_heads, preferred_element_type=jnp.float32)
    d_keys = jnp.einsum("bhqk,bqhe->bkhe", d_raw, queries, preferred_element_type=jnp.float32)
    d_values = jnp.einsum("bhqk,bqhe->bkhe", probs_low, d_grid, preferred_element_type=jnp.float32)
    d_proj = (
        jnp.stack([d_queries, d_keys, d_values], axis=2)
        .astype(jnp.bfloat16)
        .reshape(tokens, 3, local_width)
    )
    proj_local = jnp.einsum("td,tce->dce", first_in, d_proj, preferred_element_type=jnp.float32)
    first_terms = jnp.einsum("tce,dce->td", d_proj, attn_proj, preferred_element_type=jnp.float32)
    d_first = lax.psum(first_terms.astype(jnp.bfloat16), "tensor").astype(jnp.float32)
    input_grad = d_middle + norm_back(d_first, normed_one, inverse_one, attn_gain)
    attn_part = jnp.sum(d_first * normed_one, axis=0)
    proj_grad, merge_grad, router_grad, attn_gain_grad, mixer_gain_grad = lax.psum(
        (proj_local, merge_local, router_part, attn_part, mixer_part), "expert"
    )
    return (
        block_output,
        input_grad,
        attn_gain_grad,
        proj_grad,
        merge_grad,
        mixer_gain_grad,
        router_grad,
        up_local[None],
        down_local[None],
    )


def solution(mesh):
    in_specs = (
        P("expert", None),
        P(),
        P(None, None, "tensor"),
        P("tensor", None),
        P(),
        P(),
        P("expert", None, "tensor"),
        P("expert", "tensor", None),
        P("expert", None),
        P("expert", None),
        P("expert", None),
    )
    out_specs = (
        P("expert", None),
        P("expert", None),
        P(),
        P(None, None, "tensor"),
        P("tensor", None),
        P(),
        P(),
        P("expert", None, "tensor"),
        P("expert", "tensor", None),
    )
    return jax.shard_map(
        on_device, mesh=mesh, in_specs=in_specs, out_specs=out_specs, check_vma=False
    )
```

profile of v0, /device:TPU:8, one launch (start us, length us, event | category | flops | bytes accessed | tf_op | source)
XLA Modules:
  0.0 514.5 jit_solution(15176419366171153621)
XLA Ops:
  16.9 30.4 %all-reduce.9.cloned.1.call-done = bf16[197,768]{1,0:T(8,128)(2,1)} async-done(((bf16[197,768]{1,0:T(8,128)(2,1)}), bf16[197,768]{1,0:T(8,128)(2,1)}) %all-reduce.9.cloned.1.call-update) | async-done | bytes 302608 | tf_op jit(solution)/shard_map/psum | solution.py:116
  56.0 6.2 %all-to-all-start = ((bf16[8,192,768]{2,1,0:T(8,128)(2,1)}), bf16[8,192,768]{2,1,0:T(8,128)(2,1)}, u32[]{:S(2)}, u32[]{:S(2)}) async-start(bf16[8,192,768]{2,1,0:T(8,128)(2,1)} %bitcast.19), calls=%async_computation | async-start | bytes 4718592 | tf_op jit(solution)/shard_map/all_to_all | solution.py:60
  66.3 3.2 scatter_custom_fusion.1
  69.5 43.8 %all-to-all-done = bf16[8,192,768]{2,1,0:T(8,128)(2,1)} async-done(((bf16[8,192,768]{2,1,0:T(8,128)(2,1)}), bf16[8,192,768]{2,1,0:T(8,128)(2,1)}, u32[]{:S(2)}, u32[]{:S(2)}) %all-to-all-start) | async-done | bytes 2359328 | tf_op jit(solution)/shard_map/all_to_all | solution.py:60
  116.2 6.2 %all-to-all-start.2 = ((bf16[8,192,768]{2,1,0:T(8,128)(2,1)}), bf16[8,192,768]{2,1,0:T(8,128)(2,1)S(1)}, u32[]{:S(2)}, u32[]{:S(2)}) async-start(bf16[8,192,768]{2,1,0:T(8,128)(2,1)} %bitcast.27), calls=%async_computation.2 | async-start | bytes 4718592 | tf_op jit(solution)/shard_map/all_to_all | solution.py:60
  122.4 5.0 multiply_convert_fusion
  127.5 46.5 %all-to-all-done.2 = bf16[8,192,768]{2,1,0:T(8,128)(2,1)S(1)} async-done(((bf16[8,192,768]{2,1,0:T(8,128)(2,1)}), bf16[8,192,768]{2,1,0:T(8,128)(2,1)S(1)}, u32[]{:S(2)}, u32[]{:S(2)}) %all-to-all-start.2) | async-done | bytes 2359328 | tf_op jit(solution)/shard_map/all_to_all | solution.py:60
  174.0 4.3 fusion
  178.4 2.9 convolution_convert_fusion
  181.2 6.1 %all-to-all-start.3 = ((bf16[8,192,768]{2,1,0:T(8,128)(2,1)}), bf16[8,192,768]{2,1,0:T(8,128)(2,1)S(1)}, u32[]{:S(2)}, u32[]{:S(2)}) async-start(bf16[8,192,768]{2,1,0:T(8,128)(2,1)} %bitcast.139), calls=%async_computation.3 | async-start | bytes 4718592 | tf_op jit(solution)/shard_map/all_to_all | solution.py:67
  187.3 4.2 convolution_convert_fusion.1
  191.6 47.3 %all-to-all-done.3 = bf16[8,192,768]{2,1,0:T(8,128)(2,1)S(1)} async-done(((bf16[8,192,768]{2,1,0:T(8,128)(2,1)}), bf16[8,192,768]{2,1,0:T(8,128)(2,1)S(1)}, u32[]{:S(2)}, u32[]{:S(2)}) %all-to-all-start.3) | async-done | bytes 2359328 | tf_op jit(solution)/shard_map/all_to_all | solution.py:67
  240.3 6.7 %all-to-all-start.1 = ((bf16[8,192,768]{2,1,0:T(8,128)(2,1)}), bf16[8,192,768]{2,1,0:T(8,128)(2,1)}, u32[]{:S(2)}, u32[]{:S(2)}) async-start(bf16[8,192,768]{2,1,0:T(8,128)(2,1)} %bitcast.138), calls=%async_computation.1 | async-start | bytes 4718592 | tf_op jit(solution)/shard_map/all_to_all | solution.py:67
  255.4 2.9 reshape.332
  258.3 39.7 %all-to-all-done.1 = bf16[8,192,768]{2,1,0:T(8,128)(2,1)} async-done(((bf16[8,192,768]{2,1,0:T(8,128)(2,1)}), bf16[8,192,768]{2,1,0:T(8,128)(2,1)}, u32[]{:S(2)}, u32[]{:S(2)}) %all-to-all-start.1) | async-done | bytes 2359328 | tf_op jit(solution)/shard_map/all_to_all | solution.py:67
  302.8 3.0 reshape.324
  305.9 6.1 %multiply_reduce_fusion = (bf16[197,2]{1,0:T(8,128)(2,1)S(1)}, bf16[197,768]{1,0:T(8,128)(2,1)}, bf16[197,768]{1,0:T(8,128)(2,1)}) fusion(f32[197,2,768]{2,1,0:T(2,128)} %reshape.324, f32[197,768]{1,0:T(8,128)} %convert_element_type.124, f32[197,2]{1,0:T(8,128)S(1)} %copy-done.21, f32[197,2]{1,0:T(8,128)S(1)} %copy-done.19, f32[197,2,768]{2,1,0:T(2,128)S(1)} %copy-done.8), kind=kLoop, calls=%fused_computation.29 | loop fusion | flops 1815158 | bytes 3635044 | tf_op jit(solution)/shard_map/reduce_sum | solution.py:167
  312.1 6.4 %psum.73 = bf16[197,2]{0,1:T(2,128)(2,1)S(1)} all-reduce(bf16[197,2]{0,1:T(2,128)(2,1)S(1)} %copy.114), channel_id=1, replica_groups=mesh['expert'=8,'tensor'=4] {'tensor'}, use_global_device_ids=true, to_apply=%region_21.22 | all-reduce | flops 394 | bytes 1576 | tf_op jit(solution)/shard_map/psum | solution.py:170
  318.8 32.1 %all-reduce.11.cloned.1.call-done = bf16[197,768]{1,0:T(8,128)(2,1)} async-done(((bf16[197,768]{1,0:T(8,128)(2,1)}), bf16[197,768]{1,0:T(8,128)(2,1)}) %all-reduce.11.cloned.1.call-update) | async-done | bytes 302608 | tf_op jit(solution)/shard_map/psum | solution.py:169
  358.5 3.9 convolution_bitcast_fusion
  362.4 4.2 convolution_bitcast_fusion.1
  366.8 24.7 %all-reduce.15.cloned.1.call-done = (bf16[197,768]{1,0:T(8,128)(2,1)}, bf16[197,768]{1,0:T(8,128)(2,1)}) async-done(((bf16[197,768]{1,0:T(8,128)(2,1)}, bf16[197,768]{1,0:T(8,128)(2,1)}), (bf16[197,768]{1,0:T(8,128)(2,1)}, bf16[197,768]{1,0:T(8,128)(2,1)})) %all-reduce.15.cloned.1.call-update) | async-done | bytes 605200 | tf_op jit(solution)/shard_map/psum | solution.py:142
  392.9 35.9 %all-reduce.1 = (f32[768]{0:T(1024)}, f32[768]{0:T(1024)}, f32[768,4]{0,1:T(4,128)}) all-reduce(f32[768]{0:T(1024)S(1)} %get-tuple-element.14, f32[768]{0:T(1024)S(1)} %get-tuple-element.11, f32[768,4]{0,1:T(4,128)S(1)} %fusion.45), channel_id=1, replica_groups=mesh['expert'=8,'tensor'=4] {'expert'}, use_global_device_ids=true, to_apply=%region_28.29 | all-reduce | flops 4608 | bytes 36864 | tf_op jit(solution)/shard_map/psum | solution.py:214
  431.0 73.3 %all-reduce.13.cloned.1.call-done = (f32[768,3,192]{0,2,1:T(8,128)}, f32[192,768]{1,0:T(8,128)}) async-done(((f32[768,3,192]{0,2,1:T(8,128)}, f32[192,768]{1,0:T(8,128)}), (f32[768,3,192]{0,2,1:T(8,128)}, f32[192,768]{1,0:T(8,128)})) %all-reduce.13.cloned.1.call-update) | async-done | bytes 2359312 | tf_op jit(solution)/shard_map/psum | solution.py:214
  (189 shorter events, 54.6 us)
Async XLA Ops:
  7.2 40.1 %all-reduce.9.cloned.1.call-start = ((), (), s32[]{:S(2)}) async-start(), calls=%async_computation.4 | async-start | bytes 614400 | tf_op jit(solution)/shard_map/psum | solution.py:116
  11.2 36.1 %copy-start.1 = (bf16[197,768]{1,0:T(8,128)(2,1)S(1)}, bf16[197,768]{1,0:T(8,128)(2,1)}, u32[]{:S(2)}) copy-start(bf16[197,768]{1,0:T(8,128)(2,1)} %param.11) | copy-start | bytes 907780
  11.3 38.3 %copy-start.30 = (f32[768]{0:T(1024)S(1)}, f32[768]{0:T(1024)}, u32[]{:S(2)}) copy-start(f32[768]{0:T(1024)} %param.15) | copy-start | bytes 9220
  11.6 39.2 %copy-start.2 = (f32[3,197,197]{1,2,0:T(8,128)}, f32[3,197,197]{1,2,0:T(8,128)S(1)}, u32[]{:S(2)}) copy-start(f32[3,197,197]{1,2,0:T(8,128)S(1)} %get-tuple-element.32) | copy-start | bytes 1397128
  56.0 57.3 %all-to-all-start = ((bf16[8,192,768]{2,1,0:T(8,128)(2,1)}), bf16[8,192,768]{2,1,0:T(8,128)(2,1)}, u32[]{:S(2)}, u32[]{:S(2)}) async-start(bf16[8,192,768]{2,1,0:T(8,128)(2,1)} %bitcast.19), calls=%async_computation | async-start | bytes 4718592 | tf_op jit(solution)/shard_map/all_to_all | solution.py:60
  65.7 50.5 %copy-start.40 = (s32[197,1]{0,1:T(1,128)}, s32[197,1]{0,1:T(1,128)S(1)}, u32[]{:S(2)}) copy-start(s32[197,1]{0,1:T(1,128)S(1)} %get-tuple-element.29) | copy-start | bytes 2368
  65.7 50.5 %copy-start.42 = (s32[197,1]{0,1:T(1,128)}, s32[197,1]{0,1:T(1,128)S(1)}, u32[]{:S(2)}) copy-start(s32[197,1]{0,1:T(1,128)S(1)} %get-tuple-element.30) | copy-start | bytes 2368
  66.0 50.2 %copy-start.36 = (f32[197]{0:T(256)}, f32[197]{0:T(256)S(1)}, u32[]{:S(2)}) copy-start(f32[197]{0:T(256)S(1)} %add_divide_fusion) | copy-start | bytes 2368
  66.1 50.1 %copy-start.18 = (f32[197,2]{1,0:T(8,128)}, f32[197,2]{1,0:T(8,128)S(1)}, u32[]{:S(2)}) copy-start(f32[197,2]{1,0:T(8,128)S(1)} %copy.107) | copy-start | bytes 4732
  116.2 57.8 %all-to-all-start.2 = ((bf16[8,192,768]{2,1,0:T(8,128)(2,1)}), bf16[8,192,768]{2,1,0:T(8,128)(2,1)S(1)}, u32[]{:S(2)}, u32[]{:S(2)}) async-start(bf16[8,192,768]{2,1,0:T(8,128)(2,1)} %bitcast.27), calls=%async_computation.2 | async-start | bytes 4718592 | tf_op jit(solution)/shard_map/all_to_all | solution.py:60
  181.2 57.7 %all-to-all-start.3 = ((bf16[8,192,768]{2,1,0:T(8,128)(2,1)}), bf16[8,192,768]{2,1,0:T(8,128)(2,1)S(1)}, u32[]{:S(2)}, u32[]{:S(2)}) async-start(bf16[8,192,768]{2,1,0:T(8,128)(2,1)} %bitcast.139), calls=%async_computation.3 | async-start | bytes 4718592 | tf_op jit(solution)/shard_map/all_to_all | solution.py:67
  240.3 57.7 %all-to-all-start.1 = ((bf16[8,192,768]{2,1,0:T(8,128)(2,1)}), bf16[8,192,768]{2,1,0:T(8,128)(2,1)}, u32[]{:S(2)}, u32[]{:S(2)}) async-start(bf16[8,192,768]{2,1,0:T(8,128)(2,1)} %bitcast.138), calls=%async_computation.1 | async-start | bytes 4718592 | tf_op jit(solution)/shard_map/all_to_all | solution.py:67
  247.1 103.9 %all-reduce.11.cloned.1.call-start = ((), (), s32[]{:S(2)}) async-start(), calls=%async_computation.5 | async-start | bytes 614400 | tf_op jit(solution)/shard_map/psum | solution.py:169
  305.8 45.1 %copy-start.5 = (bf16[197,768]{1,0:T(8,128)(2,1)S(1)}, bf16[197,768]{1,0:T(8,128)(2,1)}, u32[]{:S(2)}) copy-start(bf16[197,768]{1,0:T(8,128)(2,1)} %all-reduce.9.cloned.1.call-done) | copy-start | bytes 907780
  305.8 45.1 %copy-start.31 = (f32[768]{0:T(1024)S(1)}, f32[768]{0:T(1024)}, u32[]{:S(2)}) copy-start(f32[768]{0:T(1024)} %param.15) | copy-start | bytes 9220
  305.8 45.1 %copy-start.35 = (f32[197]{0:T(256)S(1)}, f32[197]{0:T(256)}, u32[]{:S(2)}) copy-start(f32[197]{0:T(256)} %copy-done.34) | copy-start | bytes 2368
  305.9 45.1 %copy-start.39 = (f32[197]{0:T(256)S(1)}, f32[197]{0:T(256)}, u32[]{:S(2)}) copy-start(f32[197]{0:T(256)} %copy-done.38) | copy-start | bytes 2368
  305.9 45.1 %copy-start.41 = (s32[197,1]{0,1:T(1,128)S(1)}, s32[197,1]{0,1:T(1,128)}, u32[]{:S(2)}) copy-start(s32[197,1]{0,1:T(1,128)} %copy-done.40) | copy-start | bytes 2368
  305.9 45.1 %copy-start.43 = (s32[197,1]{0,1:T(1,128)S(1)}, s32[197,1]{0,1:T(1,128)}, u32[]{:S(2)}) copy-start(s32[197,1]{0,1:T(1,128)} %copy-done.42) | copy-start | bytes 2368
  305.9 45.1 %copy-start.45 = (bf16[768,4]{0,1:T(4,128)(2,1)S(1)}, bf16[768,4]{0,1:T(4,128)(2,1)}, u32[]{:S(2)}) copy-start(bf16[768,4]{0,1:T(4,128)(2,1)} %param.16) | copy-start | bytes 18436
  305.9 46.7 %copy-start.10 = (bf16[197,768]{1,0:T(8,128)(2,1)S(1)}, bf16[197,768]{1,0:T(8,128)(2,1)}, u32[]{:S(2)}) copy-start(bf16[197,768]{1,0:T(8,128)(2,1)} %param.21) | copy-start | bytes 907780
  312.0 40.9 %copy-start.17 = (bf16[192,768]{1,0:T(8,128)(2,1)S(1)}, bf16[192,768]{1,0:T(8,128)(2,1)}, u32[]{:S(2)}) copy-start(bf16[192,768]{1,0:T(8,128)(2,1)} %param.14) | copy-start | bytes 884740
  318.5 73.0 %all-reduce.15.cloned.1.call-start = ((), (), s32[]{:S(2)}) async-start(), calls=%async_computation.7 | async-start | bytes 1228800 | tf_op jit(solution)/shard_map/psum | solution.py:142
  356.6 147.7 %all-reduce.13.cloned.1.call-start = ((), (), s32[]{:S(2)}) async-start(), calls=%async_computation.6 | async-start | bytes 4718592 | tf_op jit(solution)/shard_map/psum | solution.py:214
  (34 other events, 131.4 us)
Sparse Core Ops, SparseCore 0:
  14.4 32.8 all-reduce.8
  318.6 32.2 all-reduce.10
  356.7 34.7 all-reduce.14
  395.5 108.7 all-reduce.12
where the time goes:
time: 518 us; the launch traced here: 515 us
  waiting for transfers between devices  338 us (65%)
  blocking collectives  42.3 us (8%)
  matrix products  34.7 us (7%)
  local copies, waits for them, and re-layouts  31.5 us (6%)
  other arithmetic  27.8 us (5%)
  starting transfers between devices  25.6 us (5%)
  between operations  14.6 us (3%)
    all_to_all x2, waiting for transfers between devices, spread_rows(): lax.all_to_all(paired, 'expert', split_axis=0, concat_axis=0, tiled=True)  90.4 us
    all_to_all x2, waiting for transfers between devices, return_rows(): lax.all_to_all(sent_rows, 'expert', split_axis=0, concat_axis=0, tiled=True)  87.1 us
    psum x1, waiting for transfers between devices, on_device(): lax.psum((proj_local, merge_local, router_part, attn_part, mixer_part), '...  73.3 us
    psum x1, blocking collectives, on_device(): lax.psum((proj_local, merge_local, router_part, attn_part, mixer_part), '...  35.9 us
    psum x1, waiting for transfers between devices, on_device(): lax.psum(d_picked.astype(jnp.bfloat16), 'tensor').astype(jnp.float32)  32.1 us
    psum x1, waiting for transfers between devices, on_device(): lax.psum(merge_terms.astype(jnp.bfloat16), 'tensor').astype(jnp.float32)  30.4 us
    psum x1, waiting for transfers between devices, on_device(): lax.psum(mixed_rows.astype(jnp.bfloat16), 'tensor').astype(jnp.float32)  24.7 us
    all_to_all x2, starting transfers between devices, return_rows(): lax.all_to_all(sent_rows, 'expert', split_axis=0, concat_axis=0, tiled=True)  12.8 us
  transfers between devices with their start and end apart: 8, of which 8 were waited for; matrix products, arithmetic and copies ran while one was open for 9% of the time, Pallas kernels for 0%

commit v1 on v0

--- a/solution.py
+++ b/solution.py
@@ -1,6 +1,10 @@
+import functools
+
 import jax
 import jax.numpy as jnp
 from jax import lax
+from jax.experimental import pallas as pl
+from jax.experimental.pallas import tpu as pltpu
 from jax.sharding import PartitionSpec as P
 
 D = 768
@@ -226,6 +230,675 @@
         down_local[None],
     )
 
+MESH = pl.DeviceIdType.MESH
+VMEM_LIMIT = 60 * 1024 * 1024
+
+
+class Net:
+    def __init__(self, sizes):
+        e = lax.axis_index("expert")
+        t = lax.axis_index("tensor")
+        self.sizes = sizes
+        self.at = [e // sizes[1], e % sizes[1], t // sizes[3], t % sizes[3]]
+
+    def shift(self, rel):
+        return [(a + r) % s if r else a for a, r, s in zip(self.at, rel, self.sizes)]
+
+    def ident(self, place):
+        return (place[0] * self.sizes[1] + place[1], place[2] * self.sizes[3] + place[3])
+
+    def peers(self, dims):
+        found = []
+        for d in dims:
+            for j in range(1, self.sizes[d]):
+                rel = [0, 0, 0, 0]
+                rel[d] = j
+                found.append(self.ident(self.shift(rel)))
+        return found
+
+    def enter(self, dims):
+        barrier = pltpu.get_barrier_semaphore()
+        near = self.peers(dims)
+        for peer in near:
+            pl.semaphore_signal(barrier, inc=1, device_id=peer, device_id_type=MESH)
+        pl.semaphore_wait(barrier, len(near))
+
+
+def slot_of(rel, sizes, dims):
+    index = 0
+    for d in dims:
+        index = index * sizes[d] + rel[d] % sizes[d]
+    return index
+
+
+def spread(net, own, out, send, recv, order):
+    sizes = net.sizes
+    dims = sorted(order)
+    sent = []
+
+    def block(rel):
+        place = net.shift(rel)
+        index = 0
+        for d in dims:
+            index = index * sizes[d] + place[d]
+        return index
+
+    def copy_of(source, rel, d, j):
+        there = list(rel)
+        there[d] = there[d] - j
+        step = [0, 0, 0, 0]
+        step[d] = j
+        return pltpu.make_async_remote_copy(
+            src_ref=source,
+            dst_ref=out.at[block(rel)],
+            send_sem=send.at[len(sent)],
+            recv_sem=recv.at[slot_of(there, sizes, dims)],
+            device_id=net.ident(net.shift(step)),
+            device_id_type=MESH,
+        )
+
+    def forward(source, rel, later):
+        for d in later:
+            for j in range(1, sizes[d]):
+                copy = copy_of(source, rel, d, j)
+                copy.start()
+                sent.append(copy)
+
+    zero = (0, 0, 0, 0)
+    forward(own, zero, order)
+    out[block(zero)] = own[...]
+    yield
+    held = [zero]
+    for k, d in enumerate(order):
+        fresh = []
+        for base in held:
+            for j in range(1, sizes[d]):
+                rel = list(base)
+                rel[d] = j
+                here = out.at[block(rel)]
+                pltpu.make_async_remote_copy(
+                    src_ref=here,
+                    dst_ref=here,
+                    send_sem=send.at[0],
+                    recv_sem=recv.at[slot_of(rel, sizes, dims)],
+                    device_id=net.peers([d])[0],
+                    device_id_type=MESH,
+                ).wait_recv()
+                forward(here, rel, order[k + 1 :])
+                fresh.append(tuple(rel))
+        held = held + fresh
+        yield
+    for copy in sent:
+        copy.wait_send()
+
+
+def together(steps):
+    live = list(steps)
+    while live:
+        left = []
+        for step in live:
+            try:
+                next(step)
+                left.append(step)
+            except StopIteration:
+                pass
+        live = left
+
+
+def count_of(sizes, order):
+    total = 1
+    for d in order:
+        total *= sizes[d]
+    return total
+
+
+def params(cid):
+    return pltpu.CompilerParams(
+        collective_id=cid, has_side_effects=True, vmem_limit_bytes=VMEM_LIMIT
+    )
+
+
+def vmem(count):
+    return [pl.BlockSpec(memory_space=pltpu.VMEM)] * count
+
+
+def gather_kernel(sizes, orders, *refs):
+    n = len(orders)
+    net = Net(sizes)
+    net.enter(sorted({d for order in orders for d in order}))
+    ins, outs, sems = refs[:n], refs[n : 2 * n], refs[2 * n :]
+    together(
+        [
+            spread(net, ins[i], outs[i], sems[2 * i], sems[2 * i + 1], orders[i])
+            for i in range(n)
+        ]
+    )
+
+
+def gather_call(sizes, cid, arrays, orders):
+    counts = [count_of(sizes, order) for order in orders]
+    sems = []
+    for count in counts:
+        sems += [pltpu.SemaphoreType.DMA((count - 1,)), pltpu.SemaphoreType.DMA((count,))]
+    return pl.pallas_call(
+        functools.partial(gather_kernel, sizes, orders),
+        out_shape=[
+            jax.ShapeDtypeStruct((count,) + a.shape, a.dtype) for count, a in zip(counts, arrays)
+        ],
+        in_specs=vmem(len(arrays)),
+        out_specs=vmem(len(arrays)),
+        scratch_shapes=sems,
+        compiler_params=params(cid),
+    )(*arrays)
+
+
+def scatter_tensor(net, terms, landed, send, recv):
+    sizes = net.sizes
+    sent = []
+    index = 0
+    for jx in range(sizes[2]):
+        for jc in range(sizes[3]):
+            if jx == 0 and jc == 0:
+                continue
+            place = net.shift((0, 0, jx, jc))
+            back = slot_of((0, 0, -jx, -jc), sizes, (2, 3)) - 1
+            copy = pltpu.make_async_remote_copy(
+                src_ref=terms.at[place[2] * sizes[3] + place[3]],
+                dst_ref=landed.at[back],
+                send_sem=send.at[index],
+                recv_sem=recv.at[back],
+                device_id=net.ident(place),
+                device_id_type=MESH,
+            )
+            copy.start()
+            sent.append((copy, back))
+            index += 1
+    return sent
+
+
+def scatter_finish(net, terms, landed, sent):
+    own = net.at[2] * net.sizes[3] + net.at[3]
+    total = terms[own].astype(jnp.float32)
+    for copy, slot in sent:
+        copy.wait()
+    for slot in range(len(sent)):
+        total = total + landed[slot].astype(jnp.float32)
+    return total
+
+
+def tensor_peers_enter(net, extra):
+    barrier = pltpu.get_barrier_semaphore()
+    near = []
+    for jx in range(net.sizes[2]):
+        for jc in range(net.sizes[3]):
+            if jx or jc:
+                near.append(net.ident(net.shift((0, 0, jx, jc))))
+    near = near + net.peers(extra)
+    for peer in near:
+        pl.semaphore_signal(barrier, inc=1, device_id=peer, device_id_type=MESH)
+    pl.semaphore_wait(barrier, len(near))
+
+
+def merge_kernel(sizes, terms, out, landed, send, recv):
+    net = Net(sizes)
+    tensor_peers_enter(net, ())
+    sent = scatter_tensor(net, terms, landed, send, recv)
+    out[...] = scatter_finish(net, terms, landed, sent)
+
+
+def merge_call(sizes, cid, terms):
+    tensor = terms.shape[0]
+    return pl.pallas_call(
+        functools.partial(merge_kernel, sizes),
+        out_shape=jax.ShapeDtypeStruct(terms.shape[1:], jnp.float32),
+        in_specs=vmem(1),
+        out_specs=pl.BlockSpec(memory_space=pltpu.VMEM),
+        scratch_shapes=[
+            pltpu.VMEM((tensor - 1,) + terms.shape[1:], terms.dtype),
+            pltpu.SemaphoreType.DMA((tensor - 1,)),
+            pltpu.SemaphoreType.DMA((tensor - 1,)),
+        ],
+        compiler_params=params(cid),
+    )(terms)
+
+
+def fold(net, part, out, core_in, core_sum, mid_in, mid_sum, low_in, low_sum, z_in, sems, x_first):
+    z, y, x, c = net.at
+    depth = net.sizes[0]
+    kind = part.dtype
+    wide = jnp.float32
+    core_peer = net.peers([3])[0]
+    first_dim, second_dim = (2, 1) if x_first else (1, 2)
+    mid_peer, low_peer = net.peers([first_dim])[0], net.peers([second_dim])[0]
+    first_at, second_at = net.at[first_dim], net.at[second_dim]
+
+    def remote(source, target, stage, index, landing, peer):
+        return pltpu.make_async_remote_copy(
+            src_ref=source,
+            dst_ref=target,
+            send_sem=sems.at[stage, 0, index],
+            recv_sem=sems.at[stage, 1, landing],
+            device_id=peer,
+            device_id_type=MESH,
+        )
+
+    zs = [(z + 1 + k) % depth if k < depth - 1 else z for k in range(depth)]
+    core, mid, low, far = [], [], [], []
+    for k in range(depth):
+        copy = remote(part.at[zs[k], :, :, 1 - c], core_in.at[k], 0, k, k, core_peer)
+        copy.start()
+        core.append(copy)
+    yield
+    for k in range(depth):
+        core[k].wait_recv()
+        core_sum[k] = (part[zs[k], :, :, c].astype(wide) + core_in[k].astype(wide)).astype(kind)
+        away = core_sum.at[k, :, 1 - first_at] if x_first else core_sum.at[k, 1 - first_at]
+        copy = remote(away, mid_in.at[k], 1, k, k, mid_peer)
+        copy.start()
+        mid.append(copy)
+    yield
+    for k in range(depth):
+        mid[k].wait_recv()
+        near = core_sum[k, :, first_at] if x_first else core_sum[k, first_at]
+        mid_sum[k] = (near.astype(wide) + mid_in[k].astype(wide)).astype(kind)
+        copy = remote(mid_sum.at[k, 1 - second_at], low_in.at[k], 2, k, k, low_peer)
+        copy.start()
+        low.append(copy)
+    yield
+    for k in range(depth):
+        low[k].wait_recv()
+        total = mid_sum[k, second_at].astype(wide) + low_in[k].astype(wide)
+        if k == depth - 1:
+            out[...] = total
+        else:
+            low_sum[k] = total.astype(kind)
+            landing = depth - k - 2
+            peer = net.ident([zs[k], y, x, c])
+            copy = remote(low_sum.at[k], z_in.at[landing], 3, k, landing, peer)
+            copy.start()
+            far.append(copy)
+    yield
+    for k in range(depth - 1):
+        far[k].wait_recv()
+    total = out[...]
+    for k in range(depth - 1):
+        total = total + z_in[k].astype(wide)
+    out[...] = total
+    for copy in core + mid + low + far:
+        copy.wait_send()
+
+
+def fold_scratch(sizes, shape, kind):
+    depth, ys, xs, cs = sizes
+    return [
+        pltpu.VMEM((depth, ys, xs) + shape, kind),
+        pltpu.VMEM((depth, ys, xs) + shape, kind),
+        pltpu.VMEM((depth, 2) + shape, kind),
+        pltpu.VMEM((depth, 2) + shape, kind),
+        pltpu.VMEM((depth,) + shape, kind),
+        pltpu.VMEM((depth - 1,) + shape, kind),
+        pltpu.VMEM((depth - 1,) + shape, kind),
+        pltpu.SemaphoreType.DMA((4, 2, depth)),
+    ]
+
+
+def fold_kernel(sizes, firsts, *refs):
+    n = len(firsts)
+    net = Net(sizes)
+    net.enter((0, 1, 2, 3))
+    ins, outs, rest = refs[:n], refs[n : 2 * n], refs[2 * n :]
+    together(
+        [
+            fold(net, ins[i], outs[i], *rest[8 * i : 8 * i + 8], firsts[i])
+            for i in range(n)
+        ]
+    )
+
+
+def fold_call(sizes, cid, arrays, firsts):
+    shaped = [a.reshape(tuple(sizes) + a.shape[1:]) for a in arrays]
+    scratch = []
+    for a in arrays:
+        scratch += fold_scratch(sizes, a.shape[1:], a.dtype)
+    return pl.pallas_call(
+        functools.partial(fold_kernel, sizes, firsts),
+        out_shape=[jax.ShapeDtypeStruct(a.shape[1:], jnp.float32) for a in arrays],
+        in_specs=vmem(len(arrays)),
+        out_specs=vmem(len(arrays)),
+        scratch_shapes=scratch,
+        compiler_params=params(cid),
+    )(*shaped)
+
+
+def tail_kernel(
+    sizes,
+    gain_row,
+    terms,
+    d_proj,
+    d_low,
+    d_middle,
+    normed,
+    inverse,
+    gain,
+    small,
+    grad_all,
+    proj_all,
+    low_all,
+    small_out,
+    landed,
+    grad_own,
+    small_in,
+    small_sum,
+    sc_send,
+    sc_recv,
+    g_send,
+    g_recv,
+    p_send,
+    p_recv,
+    l_send,
+    l_recv,
+    s_send,
+    s_recv,
+):
+    net = Net(sizes)
+    tensor_peers_enter(net, (0, 1))
+    sent = scatter_tensor(net, terms, landed, sc_send, sc_recv)
+    proj_step = spread(net, d_proj, proj_all, p_send, p_recv, (0, 1))
+    low_step = spread(net, d_low, low_all, l_send, l_recv, (0, 1, 2, 3))
+    next(proj_step)
+    next(low_step)
+    d_first = scatter_finish(net, terms, landed, sent)
+    scaled = d_first * gain[...]
+    plain = normed[...]
+    mean = jnp.mean(scaled, axis=-1, keepdims=True)
+    mixed = jnp.mean(scaled * plain, axis=-1, keepdims=True)
+    grad = d_middle[...] + inverse[...] * (scaled - mean - plain * mixed)
+    grad_own[...] = grad.astype(jnp.bfloat16)
+    grad_step = spread(net, grad_own, grad_all, g_send, g_recv, (2, 3))
+    next(grad_step)
+    part = jnp.sum(d_first * plain, axis=0, keepdims=True)
+    row = lax.broadcasted_iota(jnp.int32, small.shape, 0)
+    small_sum[0] = jnp.where(row == gain_row, part, small[...])
+    next(proj_step)
+    next(low_step)
+    stage, index = 0, 0
+    rounds = []
+    for d in (3, 2, 1, 0):
+        copies = []
+        for j in range(1, sizes[d]):
+            rel = [0, 0, 0, 0]
+            rel[d] = j
+            landing = index + sizes[d] - 1 - j
+            copy = pltpu.make_async_remote_copy(
+                src_ref=small_sum.at[stage],
+                dst_ref=small_in.at[landing],
+                send_sem=s_send.at[index + j - 1],
+                recv_sem=s_recv.at[landing],
+                device_id=net.ident(net.shift(rel)),
+                device_id_type=MESH,
+            )
+            copy.start()
+            copies.append(copy)
+        for copy in copies:
+            copy.wait_recv()
+        total = small_sum[stage]
+        for j in range(sizes[d] - 1):
+            total = total + small_in[index + j]
+        index += sizes[d] - 1
+        stage += 1
+        if stage < 4:
+            small_sum[stage] = total
+        else:
+            small_out[...] = total
+        rounds += copies
+        if stage < 3:
+            next(low_step)
+    for copy in rounds:
+        copy.wait_send()
+    together([grad_step, low_step, proj_step])
+
+
+def tail_call(sizes, cid, gain_row, terms, d_proj, d_low, d_middle, normed, inverse, gain, small):
+    experts_axis, tensor = sizes[0] * sizes[1], sizes[2] * sizes[3]
+    everyone = experts_axis * tensor
+    steps = sum(sizes) - 4
+    dma = pltpu.SemaphoreType.DMA
+    shape = d_low.shape
+    return pl.pallas_call(
+        functools.partial(tail_kernel, sizes, gain_row),
+        out_shape=[
+            jax.ShapeDtypeStruct((tensor,) + shape, jnp.bfloat16),
+            jax.ShapeDtypeStruct((experts_axis,) + d_proj.shape, jnp.bfloat16),
+            jax.ShapeDtypeStruct((everyone,) + shape, jnp.bfloat16),
+            jax.ShapeDtypeStruct(small.shape, jnp.float32),
+        ],
+        in_specs=vmem(8),
+        out_specs=vmem(4),
+        scratch_shapes=[
+            pltpu.VMEM((tensor - 1,) + shape, jnp.bfloat16),
+            pltpu.VMEM(shape, jnp.bfloat16),
+            pltpu.VMEM((steps,) + small.shape, jnp.float32),
+            pltpu.VMEM((4,) + small.shape, jnp.float32),
+            dma((tensor - 1,)),
+            dma((tensor - 1,)),
+            dma((tensor - 1,)),
+            dma((tensor,)),
+            dma((experts_axis - 1,)),
+            dma((experts_axis,)),
+            dma((everyone - 1,)),
+            dma((everyone,)),
+            dma((steps,)),
+            dma((steps,)),
+        ],
+        compiler_params=params(cid),
+    )(terms, d_proj, d_low, d_middle, normed, inverse, gain, small)
+
+
+def on_device_dense(
+    sizes,
+    block_input,
+    attn_gain,
+    attn_proj,
+    attn_merge,
+    mixer_gain,
+    router_weight,
+    expert_up,
+    expert_down,
+    routes,
+    keep_mask,
+    out_grad,
+):
+    experts_axis, tensor = sizes[0] * sizes[1], sizes[2] * sizes[3]
+    experts = experts_axis // PAIR
+    tokens = block_input.shape[0]
+    rows = -(-(-(-tokens // tensor)) // 8) * 8
+    padded = rows * tensor
+    local_width = attn_proj.shape[2]
+    heads_here = local_width // HEAD
+    score_scale = HEAD ** (-0.5)
+    start = lax.axis_index("tensor") * rows
+    low = jnp.bfloat16
+    wide = jnp.float32
+
+    def fill(array):
+        return jnp.pad(array, ((0, padded - tokens), (0, 0)))
+
+    def quarter(array):
+        return lax.dynamic_slice_in_dim(array, start, rows, axis=0)
+
+    input_q = quarter(fill(block_input)).astype(wide)
+    grad_q_low = quarter(fill(out_grad))
+    grad_q = grad_q_low.astype(wide)
+    route_q = quarter(fill(routes))
+    keep_q = quarter(fill(keep_mask))
+
+    normed_one, unused = norm_parts(block_input.astype(wide))
+    first_in = (normed_one * attn_gain).astype(low)
+    normed_q, inverse_q = norm_parts(input_q)
+    first_q = (normed_q * attn_gain).astype(low)
+    proj = jnp.einsum("td,dce->tce", first_in, attn_proj, preferred_element_type=wide).astype(low)
+    head_grid = proj.reshape(tokens, 3, heads_here, HEAD)
+    queries, key_heads, value_heads = head_grid[:, 0], head_grid[:, 1], head_grid[:, 2]
+    raw = jnp.einsum("qhe,khe->hqk", queries, key_heads, preferred_element_type=wide) * score_scale
+    row_top = jnp.max(raw, axis=-1, keepdims=True)
+    powers = jnp.exp(raw - row_top)
+    probs_wide = powers / jnp.sum(powers, axis=-1, keepdims=True)
+    probs_low = probs_wide.astype(low)
+    heads_out = jnp.einsum("hqk,khe->qhe", probs_low, value_heads, preferred_element_type=wide)
+    heads_out = heads_out.astype(low).reshape(tokens, local_width)
+    merge_terms = jnp.dot(fill(heads_out), attn_merge, preferred_element_type=wide).astype(low)
+
+    merged = merge_call(sizes, 1, merge_terms.reshape(tensor, rows, D))
+    middle = input_q + merged
+    normed_two, inverse_two = norm_parts(middle)
+    second_q = (normed_two * mixer_gain).astype(low)
+
+    codes = jnp.concatenate([route_q, keep_q], axis=1).astype(wide).T
+    codes = jnp.pad(codes, ((0, 4), (0, -rows % 128)))
+    everywhere = (0, 1, 2, 3)
+    second_all, grad_all, first_all, heads_all, codes_all = gather_call(
+        sizes,
+        2,
+        [second_q, grad_q_low, first_q, fill(heads_out), codes],
+        [everywhere, (2, 0, 1, 3), (2, 0, 1, 3), (0, 1), everywhere],
+    )
+    total = experts_axis * padded
+    arrived = second_all.reshape(total, D)
+    grads = grad_all.reshape(total, D)
+
+    label = lax.axis_index("expert") // PAIR
+    code = codes_all[:, :4, :rows].transpose(0, 2, 1).reshape(total, 4)
+    labels = jnp.arange(experts, dtype=wide)
+    pick_all = (code[:, 0:1] == labels).astype(wide) - (code[:, 1:2] == labels).astype(wide)
+    logits_all = jnp.dot(arrived, router_weight, preferred_element_type=wide)
+    gate_all = jax.nn.sigmoid(jnp.sum(logits_all * pick_all, axis=1, keepdims=True))
+    live_first = jnp.where(code[:, 0:1] == label.astype(wide), code[:, 2:3], 0.0)
+    live_second = jnp.where(code[:, 1:2] == label.astype(wide), code[:, 3:4], 0.0)
+    weight = live_first * gate_all + live_second * (1.0 - gate_all)
+    side = live_first - live_second
+
+    up, down = expert_up[0], expert_down[0]
+    pre_act = jnp.dot(arrived, up, preferred_element_type=wide)
+    hidden = gelu_value(pre_act).astype(low)
+    partial_terms = jnp.dot(hidden, down, preferred_element_type=wide)
+    moe_terms = (weight * partial_terms).astype(low)
+    dots = jnp.sum(
+        (partial_terms * grads.astype(wide)).reshape(experts_axis * tensor, rows, D), axis=2
+    ) * side.reshape(experts_axis * tensor, rows)
+    dots = jnp.broadcast_to(
+        jnp.pad(dots, ((0, 0), (0, -rows % 128)))[:, None, :],
+        (experts_axis * tensor, 8, -(-rows // 128) * 128),
+    )
+    d_rows = (weight * grads.astype(wide)).astype(low)
+    d_hidden = lax.dot_general(d_rows, down, (((1,), (1,)), ((), ())), preferred_element_type=wide)
+    down_local = lax.dot_general(
+        hidden, d_rows, (((0,), (0,)), ((), ())), preferred_element_type=wide
+    )
+    d_pre = (d_hidden * gelu_slope(pre_act)).astype(low)
+    up_local = lax.dot_general(arrived, d_pre, (((0,), (0,)), ((), ())), preferred_element_type=wide)
+    d_terms = lax.dot_general(
+        d_pre, up, (((1,), (1,)), ((), ())), preferred_element_type=wide
+    ).astype(low)
+
+    shape = (experts_axis * tensor, rows, D)
+    moe, d_moe, dots_sum = fold_call(
+        sizes,
+        3,
+        [moe_terms.reshape(shape), d_terms.reshape(shape), dots],
+        (True, False, True),
+    )
+    block_q = (middle + moe).astype(low)
+    mine = jnp.arange(experts, dtype=jnp.int32)
+    pick = (route_q[:, 0:1] == mine).astype(wide) - (route_q[:, 1:2] == mine).astype(wide)
+    logits = jnp.dot(second_q, router_weight, preferred_element_type=wide)
+    gate_first = jax.nn.sigmoid(jnp.sum(logits * pick, axis=1))
+    d_diff = dots_sum[0, :rows] * gate_first * (1.0 - gate_first)
+    d_logits = (d_diff[:, None] * pick).astype(low)
+    router_part = lax.dot_general(
+        d_logits, second_q, (((0,), (0,)), ((), ())), preferred_element_type=wide
+    )
+    d_second = d_moe + lax.dot_general(
+        d_logits, router_weight, (((1,), (1,)), ((), ())), preferred_element_type=wide
+    )
+    mixer_part = jnp.sum(d_second * normed_two, axis=0, keepdims=True)
+    d_middle = grad_q + norm_back(d_second, normed_two, inverse_two, mixer_gain)
+    d_low_q = d_middle.astype(low)
+
+    low_rows, block_rows = gather_call(sizes, 4, [d_low_q, block_q], [(2, 3), (2, 3)])
+    d_low = low_rows.reshape(padded, D)[:tokens]
+    block_output = block_rows.reshape(padded, D)[:tokens]
+
+    d_heads = lax.dot_general(
+        d_low, attn_merge, (((1,), (1,)), ((), ())), preferred_element_type=wide
+    ).astype(low)
+    d_grid = d_heads.reshape(tokens, heads_here, HEAD)
+    out_grid = heads_out.reshape(tokens, heads_here, HEAD)
+    delta = jnp.sum(d_grid.astype(wide) * out_grid.astype(wide), axis=2).T
+    d_probs = jnp.einsum("qhe,khe->hqk", d_grid, value_heads, preferred_element_type=wide)
+    d_raw = (probs_wide * (d_probs - delta[..., None]) * score_scale).astype(low)
+    d_queries = jnp.einsum("hqk,khe->qhe", d_raw, key_heads, preferred_element_type=wide)
+    d_keys = jnp.einsum("hqk,qhe->khe", d_raw, queries, preferred_element_type=wide)
+    d_values = jnp.einsum("hqk,qhe->khe", probs_low, d_grid, preferred_element_type=wide)
+    d_proj = jnp.concatenate(
+        [part.astype(low).reshape(tokens, local_width) for part in (d_queries, d_keys, d_values)],
+        axis=1,
+    )
+    d_proj = fill(d_proj)
+    flat_proj = attn_proj.reshape(D, 3 * local_width)
+    first_terms = lax.dot_general(
+        d_proj, flat_proj, (((1,), (1,)), ((), ())), preferred_element_type=wide
+    ).astype(low)
+    small = jnp.concatenate([router_part, mixer_part], axis=0)
+    small = jnp.pad(small, ((0, 1 + -(experts + 2) % 8), (0, 0)))
+    grad_rows, proj_all, low_all, small_all = tail_call(
+        sizes,
+        5,
+        experts + 1,
+        first_terms.reshape(tensor, rows, D),
+        d_proj,
+        d_low_q,
+        d_middle,
+        normed_q,
+        inverse_q,
+        attn_gain[None, :],
+        small,
+    )
+    input_grad = grad_rows.reshape(padded, D)[:tokens].astype(wide)
+    proj_grad = lax.dot_general(
+        first_all.reshape(total, D),
+        proj_all.reshape(total, 3 * local_width),
+        (((0,), (0,)), ((), ())),
+        preferred_element_type=wide,
+    ).reshape(D, 3, local_width)
+    merge_grad = lax.dot_general(
+        heads_all.reshape(total, local_width),
+        low_all.reshape(total, D),
+        (((0,), (0,)), ((), ())),
+        preferred_element_type=wide,
+    )
+    return (
+        block_output,
+        input_grad,
+        small_all[experts + 1],
+        proj_grad,
+        merge_grad,
+        small_all[experts],
+        small_all[:experts].T,
+        up_local[None],
+        down_local[None],
+    )
+
+
+def program_of(mesh):
+    experts_axis, tensor = mesh.shape["expert"], mesh.shape["tensor"]
+    if tensor != 4 or experts_axis % 2 or experts_axis < 4:
+        return on_device
+    capacity = max(8, 4 * TOK_DEV // (experts_axis // PAIR) // 8 * 8)
+    rows = -(-(-(-TOK_DEV // tensor)) // 8) * 8
+    if 4 * rows * tensor > 5 * capacity:
+        return on_device
+    return functools.partial(on_device_dense, (experts_axis // 2, 2, tensor // 2, 2))
+
 
 def solution(mesh):
     in_specs = (
@@ -253,5 +926,5 @@
         P("expert", "tensor", None),
     )
     return jax.shard_map(
-        on_device, mesh=mesh, in_specs=in_specs, out_specs=out_specs, check_vma=False
-    )
+        program_of(mesh), mesh=mesh, in_specs=in_specs, out_specs=out_specs, check_vma=False
+    )

time: 518 us -> 286 us (0.55)
  waiting for transfers between devices: 338 us -> 0 us
  Pallas kernels: 0 us -> 217 us
  blocking collectives: 42.3 us -> 0 us
  starting transfers between devices: 25.6 us -> 0 us
  local copies, waits for them, and re-layouts: 31.5 us -> 15.6 us
  other arithmetic: 27.8 us -> 12.4 us
  between operations: 14.6 us -> 1.1 us
    pallas_call x0 -> x5, Pallas kernels: none -> 217 us  [the longest x2 92.6 us: gather_call(): pl.pallas_call(functools.partial(gather_kernel, sizes, orders), out_shape...]
    all_to_all x4 -> x0, waiting for transfers between devices: 177 us -> none  [the longest x2 90.4 us: spread_rows(): lax.all_to_all(paired, 'expert', split_axis=0, concat_axis=0, tiled=True)]
    psum x4 -> x0, waiting for transfers between devices: 161 us -> none  [the longest x1 73.3 us: on_device(): lax.psum((proj_local, merge_local, router_part, attn_part, mixer_part), '...]
    psum x2 -> x0, blocking collectives: 42.3 us -> none  [the longest x1 35.9 us: on_device(): lax.psum((proj_local, merge_local, router_part, attn_part, mixer_part), '...]
    all_to_all x4 -> x0, starting transfers between devices: 25.2 us -> none  [the longest x2 12.8 us: return_rows(): lax.all_to_all(sent_rows, 'expert', split_axis=0, concat_axis=0, tiled=True)]
    reduce_sum x7 -> x1, other arithmetic: 12.2 us -> 0.05 us  [on_device_dense(): delta = jnp.sum(d_grid.astype(wide) * out_grid.astype(wide), axis=2).T]
    gather x4 -> x0, local copies, waits for them, and re-layouts: 10.9 us -> none  [the longest x2 5.52 us: on_device(): picked = expert_rows[source] * kept[:, :, None]]
    dot_general x19 -> x20, matrix products: 31.5 us -> 34 us  [the longest x1 5.44 us: on_device_dense(): lax.dot_general(first_all.reshape(total, D), proj_all.reshape(total, 3 *...]
  transfers between devices with their start and end apart: 8 -> 0, of which waited for: 8 -> 0; matrix products, arithmetic and copies ran while one was open for 9% -> 0% of each run, Pallas kernels for 0% -> 0%
where the time goes in v1:
time: 286 us; the launch traced here: 282 us
  Pallas kernels  217 us (76%)
  matrix products  35.9 us (13%)
  local copies, waits for them, and re-layouts  15.6 us (5%)
  other arithmetic  12.4 us (4%)
    pallas_call x2, Pallas kernels, gather_call(): pl.pallas_call(functools.partial(gather_kernel, sizes, orders), out_shape...  92.6 us
    pallas_call x1, Pallas kernels, tail_call(): pl.pallas_call(functools.partial(tail_kernel, sizes, gain_row), out_shape...  71.7 us
    pallas_call x1, Pallas kernels, fold_call(): pl.pallas_call(functools.partial(fold_kernel, sizes, firsts), out_shape=[...  44.5 us
    pallas_call x1, Pallas kernels, merge_call(): pl.pallas_call(functools.partial(merge_kernel, sizes), out_shape=jax.Shap...  7.83 us

profile of v1, /device:TPU:8, one launch (start us, length us, event | category | flops | bytes accessed | tf_op | source)
XLA Modules:
  0.0 281.7 jit_solution(16246859217391141493)
XLA Ops:
  5.1 1.2 fusion.18
  7.7 1.3 broadcast_in_dim.20.gain
  9.6 1.5 pad_dynamic-slice_fusion.1.refs_1_
  11.2 1.5 fusion.30
  15.2 7.8 %shard_map.178 = f32[56,768]{1,0:T(8,128)} custom-call(bf16[4,56,768]{2,1,0:T(8,128)(2,1)} %bitcast.146), custom_call_target="tpu_custom_call" | custom-call | tf_op jit(solution)/shard_map/pallas_call | solution.py:451
  23.1 1.8 fusion.39
  25.9 83.3 %shard_map.179 = (bf16[32,56,768]{2,1,0:T(8,128)(2,1)}, bf16[32,56,768]{2,1,0:T(8,128)(2,1)}, bf16[32,56,768]{2,1,0:T(8,128)(2,1)}, bf16[8,224,192]{2,1,0:T(8,128)(2,1)}, f32[32,8,128]{2,1,0:T(8,128)}) custom-call(bf16[56,768]{1,0:T(8,128)(2,1)} %copy-done.7, bf16[56,768]{1,0:T(8,128)(2,1)} %pad_dynamic-slice_fusion.1.refs_1_, ...), custom_call_target="tpu_custom_call" | custom-call | tf_op jit(solution)/shard_map/pallas_call | solution.py:383
  110.4 2.6 fusion.14
  113.2 2.5 fusion.1
  115.9 1.8 multiply_convert_fusion.1
  117.7 2.3 fusion.4
  120.0 2.6 convolution_bitcast_fusion.1
  122.7 3.2 %convolution_convert_fusion = bf16[1792,768]{1,0:T(8,128)(2,1)} fusion(bf16[1792,384]{1,0:T(8,128)(2,1)S(1)} %fusion.4, bf16[1,768,384]{2,1,0:T(8,128)(2,1)S(1)} %copy-done.15), kind=kOutput, calls=%fused_computation.9 | convolution fusion | flops 1058340864 | bytes 4718592 | tf_op jit(solution)/shard_map/dot_general | solution.py:799
  125.8 3.3 %fusion.2 = (f32[1792]{0:T(1024)S(1)}, bf16[1792,768]{1,0:T(8,128)(2,1)}, bf16[1792,768]{1,0:T(8,128)(2,1)S(1)}) fusion(bf16[32,56,768]{2,1,0:T(8,128)(2,1)S(1)} %copy-done.3, f32[1792]{0:T(1024)S(1)} %add_reduce_fusion, bf16[1792,384]{1,0:T(8,128)(2,1)S(1)} %get-tuple-element.63, bf16[1,384,768]{2,1,0:T(8,128)(2,1)S(1)} %copy-done.16), kind=kOutput, calls=%fused_computation.5 | convolution fusion | flops 1066596608 | bytes 10237952 | tf_op jit(solution)/shard_map/dot_general | solution.py:783
  129.1 2.3 convolution_bitcast_fusion
  132.2 44.5 %shard_map.180 = (f32[56,768]{1,0:T(8,128)}, f32[56,768]{1,0:T(8,128)}, f32[8,128]{1,0:T(8,128)}) custom-call(bf16[4,2,2,2,56,768]{5,4,3,2,1,0:T(8,128)(2,1)} %bitcast.140, bf16[4,2,2,2,56,768]{5,4,3,2,1,0:T(8,128)(2,1)} %bitcast.139, f32[4,2,2,2,8,128]{5,4,3,2,1,0:T(8,128)} %broadcast_in_dim.19.refs_2_), custom_call_target="tpu_custom_call" | custom-call | tf_op jit(solution)/shard_map/pallas_call | solution.py:563
  177.4 1.9 multiply_reduce_fusion.1
  180.9 9.4 %shard_map.181 = (bf16[4,56,768]{2,1,0:T(8,128)(2,1)}, bf16[4,56,768]{2,1,0:T(8,128)(2,1)}) custom-call(bf16[56,768]{1,0:T(8,128)(2,1)} %get-tuple-element.45.refs_0_.d_low, bf16[56,768]{1,0:T(8,128)(2,1)} %get-tuple-element.56.refs_1_), custom_call_target="tpu_custom_call" | custom-call | tf_op jit(solution)/shard_map/pallas_call | solution.py:383
  190.3 1.7 slice.77
  192.0 1.2 convolution_convert_fusion.6
  195.9 71.7 %shard_map.182 = (bf16[4,56,768]{2,1,0:T(8,128)(2,1)}, bf16[8,224,576]{2,1,0:T(8,128)(2,1)}, bf16[32,56,768]{2,1,0:T(8,128)(2,1)}, f32[8,768]{1,0:T(8,128)}) custom-call(bf16[4,56,768]{2,1,0:T(8,128)(2,1)} %bitcast.145, bf16[224,576]{1,0:T(8,128)(2,1)} %copy-done.4, bf16[56,768]{1,0:T(8,128)(2,1)} %get-tuple-element.45.refs_0_.d_low, ...), custom_call_target="tpu_custom_call" | custom-call | tf_op jit(solution)/shard_map/pallas_call | solution.py:667
  267.6 3.8 %fusion.54 = f32[192,768]{1,0:T(8,128)} fusion(bf16[1792,192]{1,0:T(8,128)(2,1)} %bitcast.152, bf16[1792,768]{1,0:T(8,128)(2,1)} %bitcast.142), kind=kOutput, calls=%fused_computation.132 | convolution fusion | flops 528482304 | bytes 4030464 | tf_op jit(solution)/shard_map/dot_general | solution.py:873
  271.4 2.8 %copy.42 = bf16[576,1792]{1,0:T(8,128)(2,1)} copy(bf16[576,1792]{0,1:T(8,128)(2,1)S(1)} %bitcast.143) | data formatting | bytes 4128768 | tf_op jit(solution)/shard_map/dot_general | solution.py:867
  274.2 5.4 %fusion.53 = f32[768,3,192]{0,2,1:T(8,128)} fusion(bf16[1792,768,1]{1,0,2:T(8,128)(2,1)} %bitcast.165, bf16[3,192,1792]{2,1,0:T(8,128)(2,1)} %bitcast.144), kind=kOutput, calls=%fused_computation.131 | convolution fusion | flops 1585446912 | bytes 6586368 | tf_op jit(solution)/shard_map/dot_general | solution.py:867
  (90 shorter events, 19.2 us)
Async XLA Ops:
  0.6 1.2 copy-start
  11.2 3.1 %copy-start.9 = (bf16[192,768]{1,0:T(8,128)(2,1)S(1)}, bf16[192,768]{1,0:T(8,128)(2,1)}, u32[]{:S(2)}) copy-start(bf16[192,768]{1,0:T(8,128)(2,1)} %param.14) | copy-start | bytes 884740
  12.7 10.3 %copy-start.2 = (bf16[197,768]{1,0:T(8,128)(2,1)S(1)}, bf16[197,768]{1,0:T(8,128)(2,1)}, u32[]{:S(2)}) copy-start(bf16[197,768]{1,0:T(8,128)(2,1)} %param.11) | copy-start | bytes 907780
  12.7 10.3 %copy-start.13 = (f32[768]{0:T(1024)S(1)}, f32[768]{0:T(1024)}, u32[]{:S(2)}) copy-start(f32[768]{0:T(1024)} %param.12) | copy-start | bytes 9220
  12.8 12.3 %copy-start.11 = (f32[768]{0:T(1024)S(1)}, f32[768]{0:T(1024)}, u32[]{:S(2)}) copy-start(f32[768]{0:T(1024)} %param.15) | copy-start | bytes 9220
  12.8 12.4 %copy-start.12 = (bf16[768,4]{0,1:T(4,128)(2,1)S(1)}, bf16[768,4]{0,1:T(4,128)(2,1)}, u32[]{:S(2)}) copy-start(bf16[768,4]{0,1:T(4,128)(2,1)} %param.16) | copy-start | bytes 18436
  25.2 0.6 copy-start.7
  113.2 2.6 copy-start.1
  113.2 2.7 copy-start.15
  115.9 1.8 copy-start.16
  122.7 3.2 %copy-start.3 = (bf16[32,56,768]{2,1,0:T(8,128)(2,1)S(1)}, bf16[32,56,768]{2,1,0:T(8,128)(2,1)}, u32[]{:S(2)}) copy-start(bf16[32,56,768]{2,1,0:T(8,128)(2,1)} %get-tuple-element.25) | copy-start | bytes 8257540
  132.2 47.1 %copy-start.8 = (bf16[56,768]{1,0:T(8,128)(2,1)S(1)}, bf16[56,768]{1,0:T(8,128)(2,1)}, u32[]{:S(2)}) copy-start(bf16[56,768]{1,0:T(8,128)(2,1)} %copy-done.7) | copy-start | bytes 258052
  132.2 47.3 %copy-start.6 = (bf16[197,768]{1,0:T(8,128)(2,1)S(1)}, bf16[197,768]{1,0:T(8,128)(2,1)}, u32[]{:S(2)}) copy-start(bf16[197,768]{1,0:T(8,128)(2,1)} %param.21) | copy-start | bytes 907780
  194.7 1.2 copy-start.4
  267.6 3.8 %copy-start.5 = (bf16[8,224,576]{2,1,0:T(8,128)(2,1)S(1)}, bf16[8,224,576]{2,1,0:T(8,128)(2,1)}, u32[]{:S(2)}) copy-start(bf16[8,224,576]{2,1,0:T(8,128)(2,1)} %get-tuple-element.34) | copy-start | bytes 6193156
  274.2 5.4 %copy-start.14 = (f32[8,768]{1,0:T(8,128)S(1)}, f32[8,768]{1,0:T(8,128)}, u32[]{:S(2)}) copy-start(f32[8,768]{1,0:T(8,128)} %get-tuple-element.32) | copy-start | bytes 73732
  274.2 6.7 %copy-start.10 = (bf16[4,56,768]{2,1,0:T(8,128)(2,1)S(1)}, bf16[4,56,768]{2,1,0:T(8,128)(2,1)}, u32[]{:S(2)}) copy-start(bf16[4,56,768]{2,1,0:T(8,128)(2,1)} %get-tuple-element.31) | copy-start | bytes 1032196

commit v2 on v1

--- a/solution.py
+++ b/solution.py
@@ -426,7 +426,7 @@
     return total
 
 
-def tensor_peers_enter(net, extra):
+def tensor_peers_enter(net, extra, experts=False):
     barrier = pltpu.get_barrier_semaphore()
     near = []
     for jx in range(net.sizes[2]):
@@ -434,6 +434,11 @@
             if jx or jc:
                 near.append(net.ident(net.shift((0, 0, jx, jc))))
     near = near + net.peers(extra)
+    if experts:
+        for jz in range(net.sizes[0]):
+            for jy in range(net.sizes[1]):
+                if jz or jy:
+                    near.append(net.ident(net.shift((jz, jy, 0, 0))))
     for peer in near:
         pl.semaphore_signal(barrier, inc=1, device_id=peer, device_id_type=MESH)
     pl.semaphore_wait(barrier, len(near))
@@ -570,43 +575,89 @@
     )(*shaped)
 
 
-def tail_kernel(
-    sizes,
-    gain_row,
-    terms,
-    d_proj,
-    d_low,
-    d_middle,
-    normed,
-    inverse,
-    gain,
-    small,
-    grad_all,
-    proj_all,
-    low_all,
-    small_out,
-    landed,
-    grad_own,
-    small_in,
-    small_sum,
-    sc_send,
-    sc_recv,
-    g_send,
-    g_recv,
-    p_send,
-    p_recv,
-    l_send,
-    l_recv,
-    s_send,
-    s_recv,
-):
+def ring(net, part, y_in, y_sum, z_in, total, own, out, sems, send, recv):
+    z, y, x, c = net.at
+    depth = net.sizes[0]
+    kind = part.dtype
+    wide = jnp.float32
+    y_peer = net.peers([1])[0]
+    zs = [(z + 1 + k) % depth if k < depth - 1 else z for k in range(depth)]
+    near, far = [], []
+
+    def remote(source, target, stage, index, landing, peer):
+        return pltpu.make_async_remote_copy(
+            src_ref=source,
+            dst_ref=target,
+            send_sem=sems.at[stage, 0, index],
+            recv_sem=sems.at[stage, 1, landing],
+            device_id=peer,
+            device_id_type=MESH,
+        )
+
+    for k in range(depth):
+        copy = remote(part.at[zs[k], 1 - y], y_in.at[k], 0, k, k, y_peer)
+        copy.start()
+        near.append(copy)
+    yield
+    for k in range(depth):
+        near[k].wait_recv()
+        here = part[zs[k], y].astype(wide) + y_in[k].astype(wide)
+        if k == depth - 1:
+            total[...] = here
+        else:
+            y_sum[k] = here.astype(kind)
+            landing = depth - k - 2
+            peer = net.ident([zs[k], y, x, c])
+            copy = remote(y_sum.at[k], z_in.at[landing], 1, k, landing, peer)
+            copy.start()
+            far.append(copy)
+    yield
+    for k in range(depth - 1):
+        far[k].wait_recv()
+    done = total[...]
+    for k in range(depth - 1):
+        done = done + z_in[k].astype(wide)
+    own[...] = done.astype(kind)
+    yield
+    yield from spread(net, own, out, send, recv, (0, 1))
+    for copy in near + far:
+        copy.wait_send()
+
+
+def ring_scratch(sizes, shape, kind):
+    depth = sizes[0]
+    count = depth * sizes[1]
+    return [
+        pltpu.VMEM((depth,) + shape, kind),
+        pltpu.VMEM((depth - 1,) + shape, kind),
+        pltpu.VMEM((depth - 1,) + shape, kind),
+        pltpu.VMEM(shape, jnp.float32),
+        pltpu.VMEM(shape, kind),
+        pltpu.SemaphoreType.DMA((2, 2, depth)),
+        pltpu.SemaphoreType.DMA((count - 1,)),
+        pltpu.SemaphoreType.DMA((count,)),
+    ]
+
+
+def tail_kernel(sizes, gain_row, *refs):
+    terms, d_middle, normed, inverse, gain, small, proj, merge = refs[:8]
+    grad_all, proj_all, merge_all, small_out = refs[8:12]
+    rest = refs[12:]
+    landed, grad_own, small_in, small_sum, sc_send, sc_recv, g_send, g_recv, s_send, s_recv = rest[
+        :10
+    ]
+    ring_one, ring_two = rest[10:18], rest[18:26]
     net = Net(sizes)
-    tensor_peers_enter(net, (0, 1))
+    tensor_peers_enter(net, (), True)
     sent = scatter_tensor(net, terms, landed, sc_send, sc_recv)
-    proj_step = spread(net, d_proj, proj_all, p_send, p_recv, (0, 1))
-    low_step = spread(net, d_low, low_all, l_send, l_recv, (0, 1, 2, 3))
-    next(proj_step)
-    next(low_step)
+    rings = [
+        ring(net, proj, *ring_one[:5], proj_all, *ring_one[5:]),
+        ring(net, merge, *ring_two[:5], merge_all, *ring_two[5:]),
+    ]
+    for step in rings:
+        next(step)
+    for step in rings:
+        next(step)
     d_first = scatter_finish(net, terms, landed, sent)
     scaled = d_first * gain[...]
     plain = normed[...]
@@ -614,84 +665,91 @@
     mixed = jnp.mean(scaled * plain, axis=-1, keepdims=True)
     grad = d_middle[...] + inverse[...] * (scaled - mean - plain * mixed)
     grad_own[...] = grad.astype(jnp.bfloat16)
-    grad_step = spread(net, grad_own, grad_all, g_send, g_recv, (2, 3))
-    next(grad_step)
     part = jnp.sum(d_first * plain, axis=0, keepdims=True)
     row = lax.broadcasted_iota(jnp.int32, small.shape, 0)
     small_sum[0] = jnp.where(row == gain_row, part, small[...])
-    next(proj_step)
-    next(low_step)
-    stage, index = 0, 0
-    rounds = []
-    for d in (3, 2, 1, 0):
-        copies = []
-        for j in range(1, sizes[d]):
-            rel = [0, 0, 0, 0]
-            rel[d] = j
-            landing = index + sizes[d] - 1 - j
-            copy = pltpu.make_async_remote_copy(
-                src_ref=small_sum.at[stage],
-                dst_ref=small_in.at[landing],
-                send_sem=s_send.at[index + j - 1],
-                recv_sem=s_recv.at[landing],
-                device_id=net.ident(net.shift(rel)),
-                device_id_type=MESH,
-            )
-            copy.start()
-            copies.append(copy)
-        for copy in copies:
-            copy.wait_recv()
-        total = small_sum[stage]
-        for j in range(sizes[d] - 1):
-            total = total + small_in[index + j]
-        index += sizes[d] - 1
-        stage += 1
-        if stage < 4:
-            small_sum[stage] = total
-        else:
-            small_out[...] = total
-        rounds += copies
-        if stage < 3:
-            next(low_step)
-    for copy in rounds:
+    copies = []
+
+    def exchange(stage, slot, landing, place):
+        copy = pltpu.make_async_remote_copy(
+            src_ref=small_sum.at[stage],
+            dst_ref=small_in.at[landing],
+            send_sem=s_send.at[slot],
+            recv_sem=s_recv.at[landing],
+            device_id=net.ident(place),
+            device_id_type=MESH,
+        )
+        copy.start()
+        copies.append(copy)
+        return copy
+
+    exchange(0, 0, 0, net.shift((0, 0, 0, 1))).wait_recv()
+    small_sum[1] = small_sum[0] + small_in[0]
+    exchange(1, 1, 1, net.shift((0, 0, 1, 0))).wait_recv()
+    small_sum[2] = small_sum[1] + small_in[1]
+    grad_step = spread(net, grad_own, grad_all, g_send, g_recv, (2, 3))
+    next(grad_step)
+    slot = 2
+    final = []
+    for jz in range(sizes[0]):
+        for jy in range(sizes[1]):
+            if jz or jy:
+                landing = 1 + slot_of((-jz, -jy, 0, 0), sizes, (0, 1))
+                final.append(exchange(2, slot, landing, net.shift((jz, jy, 0, 0))))
+                slot += 1
+    for step in rings:
+        next(step)
+    for step in rings:
+        next(step)
+    next(grad_step)
+    for step in rings:
+        next(step)
+    for copy in final:
+        copy.wait_recv()
+    total = small_sum[2]
+    for k in range(len(final)):
+        total = total + small_in[2 + k]
+    small_out[...] = total
+    for copy in copies:
         copy.wait_send()
-    together([grad_step, low_step, proj_step])
-
-
-def tail_call(sizes, cid, gain_row, terms, d_proj, d_low, d_middle, normed, inverse, gain, small):
+    together([grad_step] + rings)
+
+
+def tail_call(sizes, cid, gain_row, terms, d_middle, normed, inverse, gain, small, proj, merge):
     experts_axis, tensor = sizes[0] * sizes[1], sizes[2] * sizes[3]
-    everyone = experts_axis * tensor
-    steps = sum(sizes) - 4
+    steps = 1 + experts_axis
     dma = pltpu.SemaphoreType.DMA
-    shape = d_low.shape
+    shape = d_middle.shape
+    low = jnp.bfloat16
+    split = tuple(sizes[:2])
+    proj = proj.reshape(split + (proj.shape[0] // experts_axis,) + proj.shape[1:])
+    merge = merge.reshape(split + (merge.shape[0] // experts_axis,) + merge.shape[1:])
     return pl.pallas_call(
         functools.partial(tail_kernel, sizes, gain_row),
         out_shape=[
-            jax.ShapeDtypeStruct((tensor,) + shape, jnp.bfloat16),
-            jax.ShapeDtypeStruct((experts_axis,) + d_proj.shape, jnp.bfloat16),
-            jax.ShapeDtypeStruct((everyone,) + shape, jnp.bfloat16),
+            jax.ShapeDtypeStruct((tensor,) + shape, low),
+            jax.ShapeDtypeStruct((experts_axis,) + proj.shape[2:], low),
+            jax.ShapeDtypeStruct((experts_axis,) + merge.shape[2:], low),
             jax.ShapeDtypeStruct(small.shape, jnp.float32),
         ],
         in_specs=vmem(8),
         out_specs=vmem(4),
         scratch_shapes=[
-            pltpu.VMEM((tensor - 1,) + shape, jnp.bfloat16),
-            pltpu.VMEM(shape, jnp.bfloat16),
+            pltpu.VMEM((tensor - 1,) + shape, low),
+            pltpu.VMEM(shape, low),
             pltpu.VMEM((steps,) + small.shape, jnp.float32),
-            pltpu.VMEM((4,) + small.shape, jnp.float32),
+            pltpu.VMEM((3,) + small.shape, jnp.float32),
             dma((tensor - 1,)),
             dma((tensor - 1,)),
             dma((tensor - 1,)),
             dma((tensor,)),
-            dma((experts_axis - 1,)),
-            dma((experts_axis,)),
-            dma((everyone - 1,)),
-            dma((everyone,)),
             dma((steps,)),
             dma((steps,)),
-        ],
+        ]
+        + ring_scratch(sizes, proj.shape[2:], low)
+        + ring_scratch(sizes, merge.shape[2:], low),
         compiler_params=params(cid),
-    )(terms, d_proj, d_low, d_middle, normed, inverse, gain, small)
+    )(terms, d_middle, normed, inverse, gain, small, proj, merge)
 
 
 def on_device_dense(
@@ -735,7 +793,6 @@
     normed_one, unused = norm_parts(block_input.astype(wide))
     first_in = (normed_one * attn_gain).astype(low)
     normed_q, inverse_q = norm_parts(input_q)
-    first_q = (normed_q * attn_gain).astype(low)
     proj = jnp.einsum("td,dce->tce", first_in, attn_proj, preferred_element_type=wide).astype(low)
     head_grid = proj.reshape(tokens, 3, heads_here, HEAD)
     queries, key_heads, value_heads = head_grid[:, 0], head_grid[:, 1], head_grid[:, 2]
@@ -756,11 +813,11 @@
     codes = jnp.concatenate([route_q, keep_q], axis=1).astype(wide).T
     codes = jnp.pad(codes, ((0, 4), (0, -rows % 128)))
     everywhere = (0, 1, 2, 3)
-    second_all, grad_all, first_all, heads_all, codes_all = gather_call(
+    second_all, grad_all, codes_all = gather_call(
         sizes,
         2,
-        [second_q, grad_q_low, first_q, fill(heads_out), codes],
-        [everywhere, (2, 0, 1, 3), (2, 0, 1, 3), (0, 1), everywhere],
+        [second_q, grad_q_low, codes],
+        [everywhere, (0, 2, 1, 3), everywhere],
     )
     total = experts_axis * padded
     arrived = second_all.reshape(total, D)
@@ -843,39 +900,34 @@
         [part.astype(low).reshape(tokens, local_width) for part in (d_queries, d_keys, d_values)],
         axis=1,
     )
-    d_proj = fill(d_proj)
     flat_proj = attn_proj.reshape(D, 3 * local_width)
     first_terms = lax.dot_general(
-        d_proj, flat_proj, (((1,), (1,)), ((), ())), preferred_element_type=wide
+        fill(d_proj), flat_proj, (((1,), (1,)), ((), ())), preferred_element_type=wide
     ).astype(low)
     small = jnp.concatenate([router_part, mixer_part], axis=0)
     small = jnp.pad(small, ((0, 1 + -(experts + 2) % 8), (0, 0)))
-    grad_rows, proj_all, low_all, small_all = tail_call(
+    proj_local = lax.dot_general(
+        first_in, d_proj, (((0,), (0,)), ((), ())), preferred_element_type=wide
+    ).astype(low)
+    merge_local = lax.dot_general(
+        heads_out, d_low, (((0,), (0,)), ((), ())), preferred_element_type=wide
+    ).astype(low)
+    grad_rows, proj_all, merge_all, small_all = tail_call(
         sizes,
         5,
         experts + 1,
         first_terms.reshape(tensor, rows, D),
-        d_proj,
-        d_low_q,
         d_middle,
         normed_q,
         inverse_q,
         attn_gain[None, :],
         small,
+        proj_local,
+        merge_local,
     )
     input_grad = grad_rows.reshape(padded, D)[:tokens].astype(wide)
-    proj_grad = lax.dot_general(
-        first_all.reshape(total, D),
-        proj_all.reshape(total, 3 * local_width),
-        (((0,), (0,)), ((), ())),
-        preferred_element_type=wide,
-    ).reshape(D, 3, local_width)
-    merge_grad = lax.dot_general(
-        heads_all.reshape(total, local_width),
-        low_all.reshape(total, D),
-        (((0,), (0,)), ((), ())),
-        preferred_element_type=wide,
-    )
+    proj_grad = proj_all.astype(wide).reshape(D, 3, local_width)
+    merge_grad = merge_all.astype(wide).reshape(local_width, D)
     return (
         block_output,
         input_grad,

time: 286 us -> 226 us (0.79); the launches traced: 282 us -> 225 us
  Pallas kernels: 217 us -> 161 us
  matrix products: 35.9 us -> 29.3 us
  local copies, waits for them, and re-layouts: 15.6 us -> 18.6 us
    pallas_call x2, Pallas kernels: 92.6 us -> 51.3 us  [gather_call(): pl.pallas_call(functools.partial(gather_kernel, sizes, orders), out_shape...]
    pallas_call x1, Pallas kernels: 71.7 us -> 55.2 us  [tail_call(): pl.pallas_call(functools.partial(tail_kernel, sizes, gain_row), out_shape...]
    dot_general x3, matrix products: 10.4 us -> 3.61 us  [the longest x1 1.92 us: on_device_dense(): lax.dot_general(heads_out, d_low, (((0,), (0,)), ((), ())), preferred_ele...]
    reshape x4 -> x2, local copies, waits for them, and re-layouts: 0.41 us -> 4.02 us  [on_device_dense(): proj_grad = proj_all.astype(wide).reshape(D, 3, local_width)]
where the time goes in v2:
time: 226 us; the launch traced here: 225 us
  Pallas kernels  161 us (71%)
  matrix products  29.3 us (13%)
  local copies, waits for them, and re-layouts  18.6 us (8%)
  other arithmetic  15 us (7%)
    pallas_call x1, Pallas kernels, tail_call(): pl.pallas_call(functools.partial(tail_kernel, sizes, gain_row), out_shape...  55.2 us
    pallas_call x2, Pallas kernels, gather_call(): pl.pallas_call(functools.partial(gather_kernel, sizes, orders), out_shape...  51.3 us
    pallas_call x1, Pallas kernels, fold_call(): pl.pallas_call(functools.partial(fold_kernel, sizes, firsts), out_shape=[...  46.5 us
    pallas_call x1, Pallas kernels, merge_call(): pl.pallas_call(functools.partial(merge_kernel, sizes), out_shape=jax.Shap...  7.84 us

profile of v2, /device:TPU:8, one launch (start us, length us, event | category | flops | bytes accessed | tf_op | source)
XLA Modules:
  0.0 224.9 jit_solution(17008515308023484309)
XLA Ops:
  9.6 1.5 pad_dynamic-slice_fusion.1.refs_1_
  11.2 1.6 fusion.44
  14.5 7.8 %shard_map.178 = f32[56,768]{1,0:T(8,128)} custom-call(bf16[4,56,768]{2,1,0:T(8,128)(2,1)} %bitcast.139), custom_call_target="tpu_custom_call" | custom-call | tf_op jit(solution)/shard_map/pallas_call | solution.py:456
  22.4 1.8 fusion.47
  25.1 42.6 %shard_map.179 = (bf16[32,56,768]{2,1,0:T(8,128)(2,1)}, bf16[32,56,768]{2,1,0:T(8,128)(2,1)}, f32[32,8,128]{2,1,0:T(8,128)}) custom-call(bf16[56,768]{1,0:T(8,128)(2,1)} %copy-done.5, bf16[56,768]{1,0:T(8,128)(2,1)} %pad_dynamic-slice_fusion.1.refs_1_, f32[8,128]{1,0:T(8,128)} %pad.39.refs_2_), custom_call_target="tpu_custom_call" | custom-call | tf_op jit(solution)/shard_map/pallas_call | solution.py:383
  68.9 2.6 %fusion.14 = f32[1792]{0:T(1024)S(1)} fusion(bf16[1792,768]{1,0:T(8,128)(2,1)} %bitcast.130, bf16[768,4]{0,1:T(4,128)(2,1)S(1)} %copy-done.9, f32[1792]{0:T(1024)S(1)} %get-tuple-element.46, f32[1792]{0:T(1024)S(1)} %get-tuple-element.47), kind=kOutput, calls=%fused_computation.38 | convolution fusion | flops 11058432 | bytes 2780160 | tf_op jit(solution)/shard_map/dot_general | solution.py:830
  71.7 2.4 %fusion.1 = bf16[32,56,768]{2,1,0:T(8,128)(2,1)S(1)} fusion(bf16[32,56,768]{2,1,0:T(8,128)(2,1)} %get-tuple-element.23, f32[32,56]{1,0:T(8,128)S(1)} %mul.208), kind=kLoop, calls=%fused_computation.4 | loop fusion | flops 4128768 | bytes 5512192 | tf_op jit(solution)/shard_map/convert_element_type | solution.py:849
  74.4 1.8 multiply_convert_fusion.1
  76.3 2.3 %fusion.4 = bf16[1792,384]{1,0:T(8,128)(2,1)S(1)} fusion(bf16[1792,768]{1,0:T(8,128)(2,1)S(1)} %bitcast.136, f32[1792,384]{1,0:T(8,128)S(1)} %get-tuple-element.66, bf16[1,384,768]{2,1,0:T(8,128)(2,1)S(1)} %copy-done.12), kind=kOutput, calls=%fused_computation.11 | convolution fusion | flops 1063845888 | bytes 7471104 | tf_op jit(solution)/shard_map/dot_general | solution.py:850
  78.6 2.6 %convolution_bitcast_fusion.1 = f32[1,768,384]{2,1,0:T(8,128)} fusion(bf16[1792,768]{1,0:T(8,128)(2,1)S(1)} %bitcast.132, bf16[1792,384]{1,0:T(8,128)(2,1)S(1)} %fusion.4), kind=kOutput, calls=%fused_computation.21 | convolution fusion | flops 1056964608 | bytes 5308416 | tf_op jit(solution)/shard_map/dot_general | solution.py:855
  81.3 3.2 %convolution_convert_fusion = bf16[1792,768]{1,0:T(8,128)(2,1)} fusion(bf16[1792,384]{1,0:T(8,128)(2,1)S(1)} %fusion.4, bf16[1,768,384]{2,1,0:T(8,128)(2,1)S(1)} %copy-done.11), kind=kOutput, calls=%fused_computation.9 | convolution fusion | flops 1058340864 | bytes 4718592 | tf_op jit(solution)/shard_map/dot_general | solution.py:856
  84.5 3.3 %fusion.2 = (f32[1792]{0:T(1024)S(1)}, bf16[1792,768]{1,0:T(8,128)(2,1)}, bf16[1792,768]{1,0:T(8,128)(2,1)S(1)}) fusion(bf16[32,56,768]{2,1,0:T(8,128)(2,1)S(1)} %copy-done.3, f32[1792]{0:T(1024)S(1)} %add_reduce_fusion, bf16[1792,384]{1,0:T(8,128)(2,1)S(1)} %get-tuple-element.65, bf16[1,384,768]{2,1,0:T(8,128)(2,1)S(1)} %copy-done.12), kind=kOutput, calls=%fused_computation.5 | convolution fusion | flops 1066596608 | bytes 10237952 | tf_op jit(solution)/shard_map/dot_general | solution.py:840
  87.7 2.3 %convolution_bitcast_fusion = f32[1,384,768]{2,1,0:T(8,128)} fusion(bf16[1792,384]{1,0:T(8,128)(2,1)S(1)} %get-tuple-element.65, bf16[1792,768]{1,0:T(8,128)(2,1)S(1)} %get-tuple-element.56), kind=kOutput, calls=%fused_computation.20 | convolution fusion | flops 1056964608 | bytes 5308416 | tf_op jit(solution)/shard_map/dot_general | solution.py:851
  90.8 46.5 %shard_map.180 = (f32[56,768]{1,0:T(8,128)}, f32[56,768]{1,0:T(8,128)}, f32[8,128]{1,0:T(8,128)}) custom-call(bf16[4,2,2,2,56,768]{5,4,3,2,1,0:T(8,128)(2,1)} %bitcast.135, bf16[4,2,2,2,56,768]{5,4,3,2,1,0:T(8,128)(2,1)} %bitcast.134, f32[4,2,2,2,8,128]{5,4,3,2,1,0:T(8,128)} %broadcast_in_dim.19.refs_2_), custom_call_target="tpu_custom_call" | custom-call | tf_op jit(solution)/shard_map/pallas_call | solution.py:568
  138.0 1.9 multiply_reduce_fusion.1
  141.5 8.7 %shard_map.181 = (bf16[4,56,768]{2,1,0:T(8,128)(2,1)}, bf16[4,56,768]{2,1,0:T(8,128)(2,1)}) custom-call(bf16[56,768]{1,0:T(8,128)(2,1)} %get-tuple-element.50.refs_0_, bf16[56,768]{1,0:T(8,128)(2,1)} %get-tuple-element.58.refs_1_), custom_call_target="tpu_custom_call" | custom-call | tf_op jit(solution)/shard_map/pallas_call | solution.py:383
  150.3 1.7 slice.77
  153.2 1.9 convolution_convert_fusion.4
  159.2 55.2 %shard_map.182 = (bf16[4,56,768]{2,1,0:T(8,128)(2,1)}, bf16[8,96,576]{2,1,0:T(8,128)(2,1)}, bf16[8,24,768]{2,1,0:T(8,128)(2,1)}, f32[8,768]{1,0:T(8,128)}) custom-call(bf16[4,56,768]{2,1,0:T(8,128)(2,1)} %bitcast.140, f32[56,768]{1,0:T(8,128)} %get-tuple-element.51.refs_1_, f32[56,768]{1,0:T(8,128)} %get-tuple-element.57.refs_2_, f32[56,1]{1,0:T(8,128)} %copy.35.refs_3_, ...), custom_call_target="tpu_custom_call" | custom-call | tf_op jit(solution)/shard_map/pallas_call | solution.py:727
  214.4 1.4 slice_reduce_fusion.2
  217.2 1.8 slice_convert_fusion
  219.0 1.8 bitcast_convert_fusion
  220.8 2.0 copy.36
  222.9 2.0 reshape.228
  (80 shorter events, 22.8 us)
Async XLA Ops:
  0.6 1.2 copy-start
  8.9 4.5 %copy-start.7 = (bf16[192,768]{1,0:T(8,128)(2,1)S(1)}, bf16[192,768]{1,0:T(8,128)(2,1)}, u32[]{:S(2)}) copy-start(bf16[192,768]{1,0:T(8,128)(2,1)} %param.14) | copy-start | bytes 884740
  11.2 11.2 %copy-start.2 = (bf16[197,768]{1,0:T(8,128)(2,1)S(1)}, bf16[197,768]{1,0:T(8,128)(2,1)}, u32[]{:S(2)}) copy-start(bf16[197,768]{1,0:T(8,128)(2,1)} %param.11) | copy-start | bytes 907780
  12.8 11.6 %copy-start.8 = (f32[768]{0:T(1024)S(1)}, f32[768]{0:T(1024)}, u32[]{:S(2)}) copy-start(f32[768]{0:T(1024)} %param.15) | copy-start | bytes 9220
  12.8 11.7 %copy-start.9 = (bf16[768,4]{0,1:T(4,128)(2,1)S(1)}, bf16[768,4]{0,1:T(4,128)(2,1)}, u32[]{:S(2)}) copy-start(bf16[768,4]{0,1:T(4,128)(2,1)} %param.16) | copy-start | bytes 18436
  24.5 0.6 copy-start.5
  71.7 2.6 %copy-start.1 = (bf16[32,56,768]{2,1,0:T(8,128)(2,1)S(1)}, bf16[32,56,768]{2,1,0:T(8,128)(2,1)}, u32[]{:S(2)}) copy-start(bf16[32,56,768]{2,1,0:T(8,128)(2,1)} %get-tuple-element.22) | copy-start | bytes 8257540
  71.7 2.7 %copy-start.11 = (bf16[1,768,384]{2,1,0:T(8,128)(2,1)S(1)}, bf16[1,768,384]{2,1,0:T(8,128)(2,1)}, u32[]{:S(2)}) copy-start(bf16[1,768,384]{2,1,0:T(8,128)(2,1)} %param.17) | copy-start | bytes 1769476
  74.4 1.8 copy-start.12
  81.2 3.2 %copy-start.3 = (bf16[32,56,768]{2,1,0:T(8,128)(2,1)S(1)}, bf16[32,56,768]{2,1,0:T(8,128)(2,1)}, u32[]{:S(2)}) copy-start(bf16[32,56,768]{2,1,0:T(8,128)(2,1)} %get-tuple-element.23) | copy-start | bytes 8257540
  90.8 49.1 %copy-start.6 = (bf16[56,768]{1,0:T(8,128)(2,1)S(1)}, bf16[56,768]{1,0:T(8,128)(2,1)}, u32[]{:S(2)}) copy-start(bf16[56,768]{1,0:T(8,128)(2,1)} %copy-done.5) | copy-start | bytes 258052
  90.8 49.3 %copy-start.4 = (bf16[197,768]{1,0:T(8,128)(2,1)S(1)}, bf16[197,768]{1,0:T(8,128)(2,1)}, u32[]{:S(2)}) copy-start(bf16[197,768]{1,0:T(8,128)(2,1)} %param.21) | copy-start | bytes 907780
  155.4 2.0 copy-start.10

commit v3 on v2

--- a/solution.py
+++ b/solution.py
@@ -444,27 +444,87 @@
     pl.semaphore_wait(barrier, len(near))
 
 
-def merge_kernel(sizes, terms, out, landed, send, recv):
+def front_kernel(sizes, tokens, orders, *refs):
+    n = len(orders)
+    values, gain, weights, merge = refs[:4]
+    ins, rest = refs[4 : 4 + n], refs[4 + n :]
+    out, heads, proj, probs, first_in = rest[:5]
+    outs, rest = rest[5 : 5 + n], rest[5 + n :]
+    terms, landed, send, recv = rest[:4]
+    sems = rest[4:]
     net = Net(sizes)
-    tensor_peers_enter(net, ())
+    tensor_peers_enter(net, (0, 1))
+    steps = [
+        spread(net, ins[i], outs[i], sems[2 * i], sems[2 * i + 1], orders[i]) for i in range(n)
+    ]
+    for step in steps:
+        next(step)
+    wide, low = jnp.float32, jnp.bfloat16
+    normed, unused = norm_parts(values[...].astype(wide))
+    first = (normed * gain[...]).astype(low)
+    first_in[...] = first
+    proj[...] = jnp.dot(first, weights[...], preferred_element_type=wide).astype(low)
+    for step in steps:
+        next(step)
+    padded, width = values.shape[0], heads.shape[1]
+    key_live = lax.broadcasted_iota(jnp.int32, (padded, padded), 1) < tokens
+    row_live = lax.broadcasted_iota(jnp.int32, (padded, HEAD), 0) < tokens
+    for h in range(width // HEAD):
+        queries = proj[:, h * HEAD : (h + 1) * HEAD]
+        keys = proj[:, width + h * HEAD : width + (h + 1) * HEAD]
+        vals = proj[:, 2 * width + h * HEAD : 2 * width + (h + 1) * HEAD]
+        raw = lax.dot_general(
+            queries, keys, (((1,), (1,)), ((), ())), preferred_element_type=wide
+        ) * (HEAD ** (-0.5))
+        raw = jnp.where(key_live, raw, -jnp.inf)
+        powers = jnp.exp(raw - jnp.max(raw, axis=-1, keepdims=True))
+        shares = powers / jnp.sum(powers, axis=-1, keepdims=True)
+        probs[h] = shares
+        mixed = jnp.dot(shares.astype(low), vals, preferred_element_type=wide)
+        heads[:, h * HEAD : (h + 1) * HEAD] = jnp.where(row_live, mixed, 0.0).astype(low)
+    merged = jnp.dot(heads[...], merge[...], preferred_element_type=wide)
+    rows = terms.shape[1]
+    for b in range(terms.shape[0]):
+        terms[b] = merged[b * rows : (b + 1) * rows].astype(low)
     sent = scatter_tensor(net, terms, landed, send, recv)
+    for step in steps:
+        next(step)
     out[...] = scatter_finish(net, terms, landed, sent)
-
-
-def merge_call(sizes, cid, terms):
-    tensor = terms.shape[0]
+    together(steps)
+
+
+def front_call(sizes, cid, tokens, values, gain, weights, merge, arrays, orders):
+    tensor = sizes[2] * sizes[3]
+    padded, width = values.shape
+    rows = padded // tensor
+    counts = [count_of(sizes, order) for order in orders]
+    local = merge.shape[0]
+    low = jnp.bfloat16
+    dma = pltpu.SemaphoreType.DMA
+    sems = []
+    for count in counts:
+        sems += [dma((count - 1,)), dma((count,))]
     return pl.pallas_call(
-        functools.partial(merge_kernel, sizes),
-        out_shape=jax.ShapeDtypeStruct(terms.shape[1:], jnp.float32),
-        in_specs=vmem(1),
-        out_specs=pl.BlockSpec(memory_space=pltpu.VMEM),
+        functools.partial(front_kernel, sizes, tokens, orders),
+        out_shape=[
+            jax.ShapeDtypeStruct((rows, width), jnp.float32),
+            jax.ShapeDtypeStruct((padded, local), low),
+            jax.ShapeDtypeStruct((padded, 3 * local), low),
+            jax.ShapeDtypeStruct((local // HEAD, padded, padded), jnp.float32),
+            jax.ShapeDtypeStruct((padded, width), low),
+        ]
+        + [jax.ShapeDtypeStruct((count,) + a.shape, a.dtype) for count, a in zip(counts, arrays)],
+        in_specs=vmem(4 + len(arrays)),
+        out_specs=vmem(5 + len(arrays)),
         scratch_shapes=[
-            pltpu.VMEM((tensor - 1,) + terms.shape[1:], terms.dtype),
-            pltpu.SemaphoreType.DMA((tensor - 1,)),
-            pltpu.SemaphoreType.DMA((tensor - 1,)),
-        ],
+            pltpu.VMEM((tensor, rows, width), low),
+            pltpu.VMEM((tensor - 1, rows, width), low),
+            dma((tensor - 1,)),
+            dma((tensor - 1,)),
+        ]
+        + sems,
         compiler_params=params(cid),
-    )(terms)
+    )(values, gain, weights, merge, *arrays)
 
 
 def fold(net, part, out, core_in, core_sum, mid_in, mid_sum, low_in, low_sum, z_in, sems, x_first):
@@ -790,35 +850,29 @@
     route_q = quarter(fill(routes))
     keep_q = quarter(fill(keep_mask))
 
-    normed_one, unused = norm_parts(block_input.astype(wide))
-    first_in = (normed_one * attn_gain).astype(low)
     normed_q, inverse_q = norm_parts(input_q)
-    proj = jnp.einsum("td,dce->tce", first_in, attn_proj, preferred_element_type=wide).astype(low)
-    head_grid = proj.reshape(tokens, 3, heads_here, HEAD)
+    codes = jnp.concatenate([route_q, keep_q], axis=1).astype(wide).T
+    codes = jnp.pad(codes, ((0, 4), (0, -rows % 128)))
+    flat_proj = attn_proj.reshape(D, 3 * local_width)
+    merged, heads_out, proj, probs_wide, first_in, grad_all, codes_all = front_call(
+        sizes,
+        1,
+        tokens,
+        fill(block_input),
+        attn_gain[None, :],
+        flat_proj,
+        attn_merge,
+        [grad_q_low, codes],
+        [(0, 2, 1, 3), (0, 1, 2, 3)],
+    )
+    head_grid = proj.reshape(padded, 3, heads_here, HEAD)
     queries, key_heads, value_heads = head_grid[:, 0], head_grid[:, 1], head_grid[:, 2]
-    raw = jnp.einsum("qhe,khe->hqk", queries, key_heads, preferred_element_type=wide) * score_scale
-    row_top = jnp.max(raw, axis=-1, keepdims=True)
-    powers = jnp.exp(raw - row_top)
-    probs_wide = powers / jnp.sum(powers, axis=-1, keepdims=True)
     probs_low = probs_wide.astype(low)
-    heads_out = jnp.einsum("hqk,khe->qhe", probs_low, value_heads, preferred_element_type=wide)
-    heads_out = heads_out.astype(low).reshape(tokens, local_width)
-    merge_terms = jnp.dot(fill(heads_out), attn_merge, preferred_element_type=wide).astype(low)
-
-    merged = merge_call(sizes, 1, merge_terms.reshape(tensor, rows, D))
     middle = input_q + merged
     normed_two, inverse_two = norm_parts(middle)
     second_q = (normed_two * mixer_gain).astype(low)
 
-    codes = jnp.concatenate([route_q, keep_q], axis=1).astype(wide).T
-    codes = jnp.pad(codes, ((0, 4), (0, -rows % 128)))
-    everywhere = (0, 1, 2, 3)
-    second_all, grad_all, codes_all = gather_call(
-        sizes,
-        2,
-        [second_q, grad_q_low, codes],
-        [everywhere, (0, 2, 1, 3), everywhere],
-    )
+    (second_all,) = gather_call(sizes, 2, [second_q], [(0, 1, 2, 3)])
     total = experts_axis * padded
     arrived = second_all.reshape(total, D)
     grads = grad_all.reshape(total, D)
@@ -882,14 +936,14 @@
     d_low_q = d_middle.astype(low)
 
     low_rows, block_rows = gather_call(sizes, 4, [d_low_q, block_q], [(2, 3), (2, 3)])
-    d_low = low_rows.reshape(padded, D)[:tokens]
+    d_low = low_rows.reshape(padded, D)
     block_output = block_rows.reshape(padded, D)[:tokens]
 
     d_heads = lax.dot_general(
         d_low, attn_merge, (((1,), (1,)), ((), ())), preferred_element_type=wide
     ).astype(low)
-    d_grid = d_heads.reshape(tokens, heads_here, HEAD)
-    out_grid = heads_out.reshape(tokens, heads_here, HEAD)
+    d_grid = d_heads.reshape(padded, heads_here, HEAD)
+    out_grid = heads_out.reshape(padded, heads_here, HEAD)
     delta = jnp.sum(d_grid.astype(wide) * out_grid.astype(wide), axis=2).T
     d_probs = jnp.einsum("qhe,khe->hqk", d_grid, value_heads, preferred_element_type=wide)
     d_raw = (probs_wide * (d_probs - delta[..., None]) * score_scale).astype(low)
@@ -897,12 +951,11 @@
     d_keys = jnp.einsum("hqk,qhe->khe", d_raw, queries, preferred_element_type=wide)
     d_values = jnp.einsum("hqk,qhe->khe", probs_low, d_grid, preferred_element_type=wide)
     d_proj = jnp.concatenate(
-        [part.astype(low).reshape(tokens, local_width) for part in (d_queries, d_keys, d_values)],
+        [part.astype(low).reshape(padded, local_width) for part in (d_queries, d_keys, d_values)],
         axis=1,
     )
-    flat_proj = attn_proj.reshape(D, 3 * local_width)
     first_terms = lax.dot_general(
-        fill(d_proj), flat_proj, (((1,), (1,)), ((), ())), preferred_element_type=wide
+        d_proj, flat_proj, (((1,), (1,)), ((), ())), preferred_element_type=wide
     ).astype(low)
     small = jnp.concatenate([router_part, mixer_part], axis=0)
     small = jnp.pad(small, ((0, 1 + -(experts + 2) % 8), (0, 0)))

time: 226 us -> 238 us (1.053)
  Pallas kernels: 161 us -> 171 us
  local copies, waits for them, and re-layouts: 18.6 us -> 26.9 us
  other arithmetic: 15 us -> 11.5 us
  matrix products: 29.3 us -> 26.8 us
    pallas_call x1, Pallas kernels: 7.84 us -> 32.2 us  [front_call(): pl.pallas_call(functools.partial(front_kernel, sizes, tokens, orders), ou...]
    pallas_call x2, Pallas kernels: 51.3 us -> 38 us  [gather_call(): pl.pallas_call(functools.partial(gather_kernel, sizes, orders), out_shape...]
where the time goes in v3:
time: 238 us; the launch traced here: 237 us
  Pallas kernels  171 us (72%)
  local copies, waits for them, and re-layouts  26.9 us (11%)
  matrix products  26.8 us (11%)
  other arithmetic  11.5 us (5%)
    pallas_call x1, Pallas kernels, tail_call(): pl.pallas_call(functools.partial(tail_kernel, sizes, gain_row), out_shape...  56 us
    pallas_call x1, Pallas kernels, fold_call(): pl.pallas_call(functools.partial(fold_kernel, sizes, firsts), out_shape=[...  44.5 us
    pallas_call x2, Pallas kernels, gather_call(): pl.pallas_call(functools.partial(gather_kernel, sizes, orders), out_shape...  38 us
    pallas_call x1, Pallas kernels, front_call(): pl.pallas_call(functools.partial(front_kernel, sizes, tokens, orders), ou...  32.2 us

profile of v3, /device:TPU:8, one launch (start us, length us, event | category | flops | bytes accessed | tf_op | source)
XLA Modules:
  0.0 237.1 jit_solution(2100179312120258141)
XLA Ops:
  7.9 1.7 pad.28.refs_0_
  9.6 2.2 copy.28.refs_2_
  11.8 32.2 %shard_map.178 = (f32[56,768]{1,0:T(8,128)}, bf16[224,192]{1,0:T(8,128)(2,1)}, bf16[224,576]{1,0:T(8,128)(2,1)}, f32[3,224,224]{2,1,0:T(8,128)}, bf16[224,768]{1...) custom-call(bf16[224,768]{1,0:T(8,128)(2,1)} %pad.28.refs_0_, ...), custom_call_target="tpu_custom_call" | custom-call | tf_op jit(solution)/shard_map/pallas_call | solution.py:507
  46.5 1.8 fusion.30
  50.0 1.7 copy.31
  51.7 1.8 copy.30
  53.5 28.3 %shard_map.179 = bf16[32,56,768]{2,1,0:T(8,128)(2,1)} custom-call(bf16[56,768]{1,0:T(8,128)(2,1)} %copy-done.10), custom_call_target="tpu_custom_call" | custom-call | tf_op jit(solution)/shard_map/pallas_call | solution.py:383
  81.8 2.6 %fusion.11 = f32[1792]{0:T(1024)S(1)} fusion(bf16[1792,768]{1,0:T(8,128)(2,1)} %bitcast.106, bf16[768,4]{0,1:T(4,128)(2,1)} %param.16, f32[1792]{0:T(1024)S(1)} %get-tuple-element.54, f32[1792]{0:T(1024)S(1)} %copy-done.15), kind=kOutput, calls=%fused_computation.32 | convolution fusion | flops 11058432 | bytes 2780160 | tf_op jit(solution)/shard_map/dot_general | solution.py:884
  86.6 1.8 multiply_convert_fusion.1
  88.4 2.3 fusion.3
  90.7 2.6 %convolution_bitcast_fusion.1 = f32[1,768,384]{2,1,0:T(8,128)} fusion(bf16[1792,768]{1,0:T(8,128)(2,1)S(1)} %bitcast.108, bf16[1792,384]{1,0:T(8,128)(2,1)S(1)} %fusion.3), kind=kOutput, calls=%fused_computation.20 | convolution fusion | flops 1056964608 | bytes 5308416 | tf_op jit(solution)/shard_map/dot_general | solution.py:909
  93.3 3.2 %convolution_convert_fusion = bf16[1792,768]{1,0:T(8,128)(2,1)} fusion(bf16[1792,384]{1,0:T(8,128)(2,1)S(1)} %fusion.3, bf16[1,768,384]{2,1,0:T(8,128)(2,1)S(1)} %copy-done.26), kind=kOutput, calls=%fused_computation.8 | convolution fusion | flops 1058340864 | bytes 4718592 | tf_op jit(solution)/shard_map/dot_general | solution.py:910
  96.5 3.4 %fusion.1 = (f32[1792]{0:T(1024)S(1)}, bf16[1792,768]{1,0:T(8,128)(2,1)}, bf16[1792,768]{1,0:T(8,128)(2,1)S(1)}) fusion(bf16[32,56,768]{2,1,0:T(8,128)(2,1)S(1)} %copy-done.3, f32[1792]{0:T(1024)S(1)} %add_reduce_fusion, bf16[1792,384]{1,0:T(8,128)(2,1)S(1)} %get-tuple-element.71, bf16[1,384,768]{2,1,0:T(8,128)(2,1)S(1)} %copy-done), kind=kOutput, calls=%fused_computation.4 | convolution fusion | flops 1066596608 | bytes 10237952 | tf_op jit(solution)/shard_map/dot_general | solution.py:894
  99.9 2.3 convolution_bitcast_fusion
  103.1 44.5 %shard_map.180 = (f32[56,768]{1,0:T(8,128)}, f32[56,768]{1,0:T(8,128)}, f32[8,128]{1,0:T(8,128)}) custom-call(bf16[4,2,2,2,56,768]{5,4,3,2,1,0:T(8,128)(2,1)} %bitcast.111, bf16[4,2,2,2,56,768]{5,4,3,2,1,0:T(8,128)(2,1)} %bitcast.110, f32[4,2,2,2,8,128]{5,4,3,2,1,0:T(8,128)} %broadcast_in_dim.20.refs_2_), custom_call_target="tpu_custom_call" | custom-call | tf_op jit(solution)/shard_map/pallas_call | solution.py:628
  148.5 1.9 multiply_reduce_fusion.1
  151.9 9.7 %shard_map.181 = (bf16[4,56,768]{2,1,0:T(8,128)(2,1)}, bf16[4,56,768]{2,1,0:T(8,128)(2,1)}) custom-call(bf16[56,768]{1,0:T(8,128)(2,1)} %get-tuple-element.58.refs_0_, bf16[56,768]{1,0:T(8,128)(2,1)} %get-tuple-element.66.refs_1_), custom_call_target="tpu_custom_call" | custom-call | tf_op jit(solution)/shard_map/pallas_call | solution.py:383
  161.6 1.8 slice.70
  164.7 2.0 convolution_convert_fusion.3
  170.6 56.0 %shard_map.182 = (bf16[4,56,768]{2,1,0:T(8,128)(2,1)}, bf16[8,96,576]{2,1,0:T(8,128)(2,1)}, bf16[8,24,768]{2,1,0:T(8,128)(2,1)}, f32[8,768]{1,0:T(8,128)}) custom-call(bf16[4,56,768]{2,1,0:T(8,128)(2,1)} %bitcast.125, f32[56,768]{1,0:T(8,128)} %get-tuple-element.59.refs_1_, f32[56,768]{1,0:T(8,128)} %get-tuple-element.65.refs_2_, f32[56,1]{1,0:T(8,128)} %copy.33.refs_3_, ...), custom_call_target="tpu_custom_call" | custom-call | tf_op jit(solution)/shard_map/pallas_call | solution.py:787
  229.4 1.8 slice_convert_fusion
  231.3 1.8 bitcast_convert_fusion
  233.1 2.0 copy.34
  235.1 2.0 reshape.209
  (105 shorter events, 24.4 us)
Async XLA Ops:
  0.6 87.7 %copy-start = (bf16[1,384,768]{2,1,0:T(8,128)(2,1)S(1)}, bf16[1,384,768]{2,1,0:T(8,128)(2,1)}, u32[]{:S(2)}) copy-start(bf16[1,384,768]{2,1,0:T(8,128)(2,1)} %param.18) | copy-start | bytes 1769476
  1.8 44.7 %copy-start.2 = (bf16[197,768]{1,0:T(8,128)(2,1)S(1)}, bf16[197,768]{1,0:T(8,128)(2,1)}, u32[]{:S(2)}) copy-start(bf16[197,768]{1,0:T(8,128)(2,1)} %param.11) | copy-start | bytes 907780
  3.7 44.8 %copy-start.22 = (s32[56]{0:T(128)}, s32[56]{0:T(128)S(1)}, u32[]{:S(2)}) copy-start(s32[56]{0:T(128)S(1)} %get-tuple-element.67) | copy-start | bytes 676
  3.7 44.8 %copy-start.24 = (s32[56]{0:T(128)}, s32[56]{0:T(128)S(1)}, u32[]{:S(2)}) copy-start(s32[56]{0:T(128)S(1)} %get-tuple-element.68) | copy-start | bytes 676
  7.9 40.6 %copy-start.14 = (f32[768]{0:T(1024)S(1)}, f32[768]{0:T(1024)}, u32[]{:S(2)}) copy-start(f32[768]{0:T(1024)} %param.15) | copy-start | bytes 9220
  9.6 39.6 %copy-start.16 = (bf16[768,4]{0,1:T(4,128)(2,1)S(1)}, bf16[768,4]{0,1:T(4,128)(2,1)}, u32[]{:S(2)}) copy-start(bf16[768,4]{0,1:T(4,128)(2,1)} %param.16) | copy-start | bytes 18436
  48.3 5.2 %copy-start.18 = (f32[56]{0:T(128)}, f32[56]{0:T(128)S(1)}, u32[]{:S(2)}) copy-start(f32[56]{0:T(128)S(1)} %broadcast_multiply_fusion.3) | copy-start | bytes 676
  48.5 5.0 %copy-start.20 = (f32[56]{0:T(128)}, f32[56]{0:T(128)S(1)}, u32[]{:S(2)}) copy-start(f32[56]{0:T(128)S(1)} %add_rsqrt_fusion.1) | copy-start | bytes 676
  53.5 28.3 %copy-start.15 = (f32[1792]{0:T(1024)S(1)}, f32[1792]{0:T(1024)}, u32[]{:S(2)}) copy-start(f32[1792]{0:T(1024)} %get-tuple-element.55) | copy-start | bytes 21508
  53.5 31.1 %copy-start.3 = (bf16[32,56,768]{2,1,0:T(8,128)(2,1)S(1)}, bf16[32,56,768]{2,1,0:T(8,128)(2,1)}, u32[]{:S(2)}) copy-start(bf16[32,56,768]{2,1,0:T(8,128)(2,1)} %get-tuple-element.27) | copy-start | bytes 8257540
  103.0 44.6 %copy-start.28 = (f32[56]{0:T(128)S(1)}, f32[56]{0:T(128)}, u32[]{:S(2)}) copy-start(f32[56]{0:T(128)} %fusion.12) | copy-start | bytes 676
  103.0 45.4 %copy-start.17 = (bf16[768,4]{0,1:T(4,128)(2,1)S(1)}, bf16[768,4]{0,1:T(4,128)(2,1)}, u32[]{:S(2)}) copy-start(bf16[768,4]{0,1:T(4,128)(2,1)} %param.16) | copy-start | bytes 18436
  103.0 45.4 %copy-start.19 = (f32[56]{0:T(128)S(1)}, f32[56]{0:T(128)}, u32[]{:S(2)}) copy-start(f32[56]{0:T(128)} %copy-done.18) | copy-start | bytes 676
  103.0 45.4 %copy-start.21 = (f32[56]{0:T(128)S(1)}, f32[56]{0:T(128)}, u32[]{:S(2)}) copy-start(f32[56]{0:T(128)} %copy-done.20) | copy-start | bytes 676
  103.0 45.4 %copy-start.23 = (s32[56]{0:T(128)S(1)}, s32[56]{0:T(128)}, u32[]{:S(2)}) copy-start(s32[56]{0:T(128)} %copy-done.22) | copy-start | bytes 676
  103.0 45.4 %copy-start.25 = (s32[56]{0:T(128)S(1)}, s32[56]{0:T(128)}, u32[]{:S(2)}) copy-start(s32[56]{0:T(128)} %copy-done.24) | copy-start | bytes 676
  103.0 47.3 %copy-start.11 = (bf16[56,768]{1,0:T(8,128)(2,1)S(1)}, bf16[56,768]{1,0:T(8,128)(2,1)}, u32[]{:S(2)}) copy-start(bf16[56,768]{1,0:T(8,128)(2,1)} %copy-done.10) | copy-start | bytes 258052
  103.0 47.5 %copy-start.5 = (bf16[197,768]{1,0:T(8,128)(2,1)S(1)}, bf16[197,768]{1,0:T(8,128)(2,1)}, u32[]{:S(2)}) copy-start(bf16[197,768]{1,0:T(8,128)(2,1)} %param.21) | copy-start | bytes 907780
  103.1 60.4 %copy-start.7 = (bf16[192,768]{1,0:T(8,128)(2,1)S(1)}, bf16[192,768]{1,0:T(8,128)(2,1)}, u32[]{:S(2)}) copy-start(bf16[192,768]{1,0:T(8,128)(2,1)} %refs_3_.1) | copy-start | bytes 884740
  147.6 17.1 %copy-start.12 = (bf16[224,192]{1,0:T(8,128)(2,1)S(1)}, bf16[224,192]{1,0:T(8,128)(2,1)}, u32[]{:S(2)}) copy-start(bf16[224,192]{1,0:T(8,128)(2,1)} %get-tuple-element.35) | copy-start | bytes 258052
  147.6 19.1 %copy-start.9 = (f32[224,192]{0,1:T(8,128)S(1)}, f32[224,192]{0,1:T(8,128)}, u32[]{:S(2)}) copy-start(f32[224,192]{0,1:T(8,128)} %copy.31) | copy-start | bytes 516100
  147.6 19.1 %copy-start.4 = (f32[3,224,224]{2,1,0:T(8,128)S(1)}, f32[3,224,224]{2,1,0:T(8,128)}, u32[]{:S(2)}) copy-start(f32[3,224,224]{2,1,0:T(8,128)} %get-tuple-element.33) | copy-start | bytes 1806340
  147.6 19.3 %copy-start.6 = (bf16[224,576]{0,1:T(8,128)(2,1)S(1)}, bf16[224,576]{0,1:T(8,128)(2,1)}, u32[]{:S(2)}) copy-start(bf16[224,576]{0,1:T(8,128)(2,1)} %copy.30) | copy-start | bytes 774148
  161.6 6.0 %copy-start.8 = (bf16[768,3,192]{0,2,1:T(8,128)(2,1)S(1)}, bf16[768,3,192]{0,2,1:T(8,128)(2,1)}, u32[]{:S(2)}) copy-start(bf16[768,3,192]{0,2,1:T(8,128)(2,1)} %param.13) | copy-start | bytes 2654212
  (5 other events, 8.9 us)

commit v4 on v2

--- a/solution.py
+++ b/solution.py
@@ -271,7 +271,7 @@
     return index
 
 
-def spread(net, own, out, send, recv, order):
+def spread(net, own, out, send, recv, order, fine=False):
     sizes = net.sizes
     dims = sorted(order)
     sent = []
@@ -326,6 +326,8 @@
                 ).wait_recv()
                 forward(here, rel, order[k + 1 :])
                 fresh.append(tuple(rel))
+                if fine:
+                    yield
         held = held + fresh
         yield
     for copy in sent:
@@ -369,7 +371,7 @@
     ins, outs, sems = refs[:n], refs[n : 2 * n], refs[2 * n :]
     together(
         [
-            spread(net, ins[i], outs[i], sems[2 * i], sems[2 * i + 1], orders[i])
+            spread(net, ins[i], outs[i], sems[2 * i], sems[2 * i + 1], orders[i], True)
             for i in range(n)
         ]
     )
@@ -501,27 +503,31 @@
         copy = remote(away, mid_in.at[k], 1, k, k, mid_peer)
         copy.start()
         mid.append(copy)
-    yield
-    for k in range(depth):
-        mid[k].wait_recv()
-        near = core_sum[k, :, first_at] if x_first else core_sum[k, first_at]
-        mid_sum[k] = (near.astype(wide) + mid_in[k].astype(wide)).astype(kind)
-        copy = remote(mid_sum.at[k, 1 - second_at], low_in.at[k], 2, k, k, low_peer)
-        copy.start()
-        low.append(copy)
-    yield
-    for k in range(depth):
-        low[k].wait_recv()
-        total = mid_sum[k, second_at].astype(wide) + low_in[k].astype(wide)
-        if k == depth - 1:
-            out[...] = total
-        else:
-            low_sum[k] = total.astype(kind)
-            landing = depth - k - 2
-            peer = net.ident([zs[k], y, x, c])
-            copy = remote(low_sum.at[k], z_in.at[landing], 3, k, landing, peer)
+        yield
+    for lead in range(depth + 1):
+        if lead < depth:
+            k = lead
+            mid[k].wait_recv()
+            near = core_sum[k, :, first_at] if x_first else core_sum[k, first_at]
+            mid_sum[k] = (near.astype(wide) + mid_in[k].astype(wide)).astype(kind)
+            copy = remote(mid_sum.at[k, 1 - second_at], low_in.at[k], 2, k, k, low_peer)
             copy.start()
-            far.append(copy)
+            low.append(copy)
+            yield
+        if lead > 0:
+            k = lead - 1
+            low[k].wait_recv()
+            total = mid_sum[k, second_at].astype(wide) + low_in[k].astype(wide)
+            if k == depth - 1:
+                out[...] = total
+            else:
+                low_sum[k] = total.astype(kind)
+                landing = depth - k - 2
+                peer = net.ident([zs[k], y, x, c])
+                copy = remote(low_sum.at[k], z_in.at[landing], 3, k, landing, peer)
+                copy.start()
+                far.append(copy)
+            yield
     yield
     for k in range(depth - 1):
         far[k].wait_recv()

time: 226 us -> 226 us (level)
  no operation moved by 1% of the time
where the time goes in v4:
time: 226 us; the launch traced here: 225 us
  Pallas kernels  162 us (72%)
  matrix products  29.3 us (13%)
  local copies, waits for them, and re-layouts  18.6 us (8%)
  other arithmetic  15 us (7%)
    pallas_call x1, Pallas kernels, tail_call(): pl.pallas_call(functools.partial(tail_kernel, sizes, gain_row), out_shape...  54.2 us
    pallas_call x2, Pallas kernels, gather_call(): pl.pallas_call(functools.partial(gather_kernel, sizes, orders), out_shape...  53.3 us
    pallas_call x1, Pallas kernels, fold_call(): pl.pallas_call(functools.partial(fold_kernel, sizes, firsts), out_shape=[...  46.2 us
    pallas_call x1, Pallas kernels, merge_call(): pl.pallas_call(functools.partial(merge_kernel, sizes), out_shape=jax.Shap...  7.84 us

profile of v4, /device:TPU:8, one launch (start us, length us, event | category | flops | bytes accessed | tf_op | source)
XLA Modules:
  0.0 225.5 jit_solution(1123276226021605610)
XLA Ops:
  9.6 1.5 pad_dynamic-slice_fusion.1.refs_1_
  11.2 1.6 fusion.44
  14.5 7.8 %shard_map.178 = f32[56,768]{1,0:T(8,128)} custom-call(bf16[4,56,768]{2,1,0:T(8,128)(2,1)} %bitcast.139), custom_call_target="tpu_custom_call" | custom-call | tf_op jit(solution)/shard_map/pallas_call | solution.py:458
  22.4 1.8 fusion.47
  25.1 44.2 %shard_map.179 = (bf16[32,56,768]{2,1,0:T(8,128)(2,1)}, bf16[32,56,768]{2,1,0:T(8,128)(2,1)}, f32[32,8,128]{2,1,0:T(8,128)}) custom-call(bf16[56,768]{1,0:T(8,128)(2,1)} %copy-done.5, bf16[56,768]{1,0:T(8,128)(2,1)} %pad_dynamic-slice_fusion.1.refs_1_, f32[8,128]{1,0:T(8,128)} %pad.39.refs_2_), custom_call_target="tpu_custom_call" | custom-call | tf_op jit(solution)/shard_map/pallas_call | solution.py:385
  70.6 2.6 %fusion.14 = f32[1792]{0:T(1024)S(1)} fusion(bf16[1792,768]{1,0:T(8,128)(2,1)} %bitcast.130, bf16[768,4]{0,1:T(4,128)(2,1)S(1)} %copy-done.9, f32[1792]{0:T(1024)S(1)} %get-tuple-element.46, f32[1792]{0:T(1024)S(1)} %get-tuple-element.47), kind=kOutput, calls=%fused_computation.38 | convolution fusion | flops 11058432 | bytes 2780160 | tf_op jit(solution)/shard_map/dot_general | solution.py:836
  73.4 2.4 %fusion.1 = bf16[32,56,768]{2,1,0:T(8,128)(2,1)S(1)} fusion(bf16[32,56,768]{2,1,0:T(8,128)(2,1)} %get-tuple-element.23, f32[32,56]{1,0:T(8,128)S(1)} %mul.208), kind=kLoop, calls=%fused_computation.4 | loop fusion | flops 4128768 | bytes 5512192 | tf_op jit(solution)/shard_map/convert_element_type | solution.py:855
  76.1 1.8 multiply_convert_fusion.1
  77.9 2.3 %fusion.4 = bf16[1792,384]{1,0:T(8,128)(2,1)S(1)} fusion(bf16[1792,768]{1,0:T(8,128)(2,1)S(1)} %bitcast.136, f32[1792,384]{1,0:T(8,128)S(1)} %get-tuple-element.66, bf16[1,384,768]{2,1,0:T(8,128)(2,1)S(1)} %copy-done.12), kind=kOutput, calls=%fused_computation.11 | convolution fusion | flops 1063845888 | bytes 7471104 | tf_op jit(solution)/shard_map/dot_general | solution.py:856
  80.2 2.6 %convolution_bitcast_fusion.1 = f32[1,768,384]{2,1,0:T(8,128)} fusion(bf16[1792,768]{1,0:T(8,128)(2,1)S(1)} %bitcast.132, bf16[1792,384]{1,0:T(8,128)(2,1)S(1)} %fusion.4), kind=kOutput, calls=%fused_computation.21 | convolution fusion | flops 1056964608 | bytes 5308416 | tf_op jit(solution)/shard_map/dot_general | solution.py:861
  82.9 3.2 %convolution_convert_fusion = bf16[1792,768]{1,0:T(8,128)(2,1)} fusion(bf16[1792,384]{1,0:T(8,128)(2,1)S(1)} %fusion.4, bf16[1,768,384]{2,1,0:T(8,128)(2,1)S(1)} %copy-done.11), kind=kOutput, calls=%fused_computation.9 | convolution fusion | flops 1058340864 | bytes 4718592 | tf_op jit(solution)/shard_map/dot_general | solution.py:862
  86.1 3.3 %fusion.2 = (f32[1792]{0:T(1024)S(1)}, bf16[1792,768]{1,0:T(8,128)(2,1)}, bf16[1792,768]{1,0:T(8,128)(2,1)S(1)}) fusion(bf16[32,56,768]{2,1,0:T(8,128)(2,1)S(1)} %copy-done.3, f32[1792]{0:T(1024)S(1)} %add_reduce_fusion, bf16[1792,384]{1,0:T(8,128)(2,1)S(1)} %get-tuple-element.65, bf16[1,384,768]{2,1,0:T(8,128)(2,1)S(1)} %copy-done.12), kind=kOutput, calls=%fused_computation.5 | convolution fusion | flops 1066596608 | bytes 10237952 | tf_op jit(solution)/shard_map/dot_general | solution.py:846
  89.4 2.3 %convolution_bitcast_fusion = f32[1,384,768]{2,1,0:T(8,128)} fusion(bf16[1792,384]{1,0:T(8,128)(2,1)S(1)} %get-tuple-element.65, bf16[1792,768]{1,0:T(8,128)(2,1)S(1)} %get-tuple-element.56), kind=kOutput, calls=%fused_computation.20 | convolution fusion | flops 1056964608 | bytes 5308416 | tf_op jit(solution)/shard_map/dot_general | solution.py:857
  92.4 46.2 %shard_map.180 = (f32[56,768]{1,0:T(8,128)}, f32[56,768]{1,0:T(8,128)}, f32[8,128]{1,0:T(8,128)}) custom-call(bf16[4,2,2,2,56,768]{5,4,3,2,1,0:T(8,128)(2,1)} %bitcast.135, bf16[4,2,2,2,56,768]{5,4,3,2,1,0:T(8,128)(2,1)} %bitcast.134, f32[4,2,2,2,8,128]{5,4,3,2,1,0:T(8,128)} %broadcast_in_dim.19.refs_2_), custom_call_target="tpu_custom_call" | custom-call | tf_op jit(solution)/shard_map/pallas_call | solution.py:574
  139.3 1.9 multiply_reduce_fusion.1
  142.8 9.1 %shard_map.181 = (bf16[4,56,768]{2,1,0:T(8,128)(2,1)}, bf16[4,56,768]{2,1,0:T(8,128)(2,1)}) custom-call(bf16[56,768]{1,0:T(8,128)(2,1)} %get-tuple-element.50.refs_0_, bf16[56,768]{1,0:T(8,128)(2,1)} %get-tuple-element.58.refs_1_), custom_call_target="tpu_custom_call" | custom-call | tf_op jit(solution)/shard_map/pallas_call | solution.py:385
  151.9 1.7 slice.77
  154.8 1.9 convolution_convert_fusion.4
  160.9 54.2 %shard_map.182 = (bf16[4,56,768]{2,1,0:T(8,128)(2,1)}, bf16[8,96,576]{2,1,0:T(8,128)(2,1)}, bf16[8,24,768]{2,1,0:T(8,128)(2,1)}, f32[8,768]{1,0:T(8,128)}) custom-call(bf16[4,56,768]{2,1,0:T(8,128)(2,1)} %bitcast.140, f32[56,768]{1,0:T(8,128)} %get-tuple-element.51.refs_1_, f32[56,768]{1,0:T(8,128)} %get-tuple-element.57.refs_2_, f32[56,1]{1,0:T(8,128)} %copy.35.refs_3_, ...), custom_call_target="tpu_custom_call" | custom-call | tf_op jit(solution)/shard_map/pallas_call | solution.py:733
  215.0 1.4 slice_reduce_fusion.2
  217.8 1.8 slice_convert_fusion
  219.6 1.8 bitcast_convert_fusion
  221.4 2.0 copy.36
  223.5 2.0 reshape.228
  (80 shorter events, 22.8 us)
Async XLA Ops:
  0.6 1.2 copy-start
  8.9 4.5 %copy-start.7 = (bf16[192,768]{1,0:T(8,128)(2,1)S(1)}, bf16[192,768]{1,0:T(8,128)(2,1)}, u32[]{:S(2)}) copy-start(bf16[192,768]{1,0:T(8,128)(2,1)} %param.14) | copy-start | bytes 884740
  11.2 11.2 %copy-start.2 = (bf16[197,768]{1,0:T(8,128)(2,1)S(1)}, bf16[197,768]{1,0:T(8,128)(2,1)}, u32[]{:S(2)}) copy-start(bf16[197,768]{1,0:T(8,128)(2,1)} %param.11) | copy-start | bytes 907780
  12.8 11.6 %copy-start.8 = (f32[768]{0:T(1024)S(1)}, f32[768]{0:T(1024)}, u32[]{:S(2)}) copy-start(f32[768]{0:T(1024)} %param.15) | copy-start | bytes 9220
  12.8 11.7 %copy-start.9 = (bf16[768,4]{0,1:T(4,128)(2,1)S(1)}, bf16[768,4]{0,1:T(4,128)(2,1)}, u32[]{:S(2)}) copy-start(bf16[768,4]{0,1:T(4,128)(2,1)} %param.16) | copy-start | bytes 18436
  24.5 0.6 copy-start.5
  73.4 2.6 %copy-start.1 = (bf16[32,56,768]{2,1,0:T(8,128)(2,1)S(1)}, bf16[32,56,768]{2,1,0:T(8,128)(2,1)}, u32[]{:S(2)}) copy-start(bf16[32,56,768]{2,1,0:T(8,128)(2,1)} %get-tuple-element.22) | copy-start | bytes 8257540
  73.4 2.7 %copy-start.11 = (bf16[1,768,384]{2,1,0:T(8,128)(2,1)S(1)}, bf16[1,768,384]{2,1,0:T(8,128)(2,1)}, u32[]{:S(2)}) copy-start(bf16[1,768,384]{2,1,0:T(8,128)(2,1)} %param.17) | copy-start | bytes 1769476
  76.1 1.8 copy-start.12
  82.9 3.2 %copy-start.3 = (bf16[32,56,768]{2,1,0:T(8,128)(2,1)S(1)}, bf16[32,56,768]{2,1,0:T(8,128)(2,1)}, u32[]{:S(2)}) copy-start(bf16[32,56,768]{2,1,0:T(8,128)(2,1)} %get-tuple-element.23) | copy-start | bytes 8257540
  92.4 48.8 %copy-start.6 = (bf16[56,768]{1,0:T(8,128)(2,1)S(1)}, bf16[56,768]{1,0:T(8,128)(2,1)}, u32[]{:S(2)}) copy-start(bf16[56,768]{1,0:T(8,128)(2,1)} %copy-done.5) | copy-start | bytes 258052
  92.4 48.9 %copy-start.4 = (bf16[197,768]{1,0:T(8,128)(2,1)S(1)}, bf16[197,768]{1,0:T(8,128)(2,1)}, u32[]{:S(2)}) copy-start(bf16[197,768]{1,0:T(8,128)(2,1)} %param.21) | copy-start | bytes 907780
  157.0 2.0 copy-start.10
